TPU v7x, 32 devices: a whole 2x2x4 slice. The times are simulated.
32 devices in a mesh: groups: 2 (over x), tile: 16 (over z, y, core).
Axes of the slice: x: 2, y: 2, z: 4, core: 2. Of those that a mesh axis runs over, the one named last changes fastest.
Arguments:
- exposures: float32 [32, 8, 256, 256], P(('groups', 'tile')), parts along dimension 0, may hold values from -2400 to 2400
- row_taps: bfloat16 [5, 21], replicated, may hold values from -1.25 to 1.25
- col_taps: bfloat16 [5, 21], replicated, may hold values from -1.25 to 1.25
- kernel_coeffs: float32 [32, 8, 25, 6], P(('groups', 'tile')), parts along dimension 0, may hold values from -1.25 to 1.25
- subpixel: float32 [32, 8, 2], P(('groups', 'tile')), parts along dimension 0, may hold values from 0.1 to 0.9
- destination: int32 [32, 32], P('groups'), parts along dimension 0, may hold values from 0 to 63, as said below
Outputs:
- significance: float32 [32, 8, 4, 128, 128], P(('groups', 'tile')), parts along dimension 0
There are 2 independent parts, one for each index of `groups`. A program takes and returns all parts, laid end to end along the dimension named above; an argument that names none is the same for every part. Nothing has to cross between parts.
Inputs may be any that keep to these rules, and one draw needn't show every extreme that they name: `destination`: entry [t, v * 4 + i] is the sky slot of block i of visit v of tile t; the slots o * 4 to (o + 1) * 4 - 1 are the patches of tile index o. Of the blocks of the 1 tiles of one tile index, at most 2 name slots of one tile index, and in every draw some tile index receives exactly 2 blocks from every tile index.
All inputs are finite; a program needn't handle non-finite values.
Results may differ from a plain program's by a relative error of at most 0.0062.
Values sent between devices are 32-bit elements; how exact they have to be, the bound alone decides.
No kernel may reach another device: no remote copies, remote signals or barrier semaphores. Data moves between devices by JAX's collectives and lax.ppermute only.
A program may use at most 128 MiB of HBM per device.

v0:
```python
import functools
import jax
import jax.numpy as jnp
from jax import lax
from jax.experimental import pallas as pl
from jax.experimental.pallas import tpu as pltpu
from jax.sharding import PartitionSpec as P


BLOCK = 128
LANES = 128
SEG = 32


def skew(rows8, base):
    base = base % LANES
    if base > LANES - 8:
        rows8 = pltpu.roll(rows8, 8, 1)
        base -= 8
    return pltpu.roll(rows8, base, 1, stride=1, stride_axis=0)


def iotas(rows):
    lane = lax.broadcasted_iota(jnp.int32, (rows, LANES), 1)
    row = lax.broadcasted_iota(jnp.int32, (rows, LANES), 0)
    return lane, lane - row


def split(x):
    high = x.astype(jnp.bfloat16)
    low = (x - high.astype(jnp.float32)).astype(jnp.bfloat16)
    return high, low


def banded_rows(tap_row, length, taps, first):
    _, diff = iotas(8)
    wide = jnp.broadcast_to(tap_row, (8, LANES))
    tiles = []
    for start in range(0, length, 8):
        rolled = skew(wide, start + first)
        cols = []
        for tile in range(length // LANES):
            k = diff + (LANES * tile - start - first)
            cols.append(jnp.where((k >= 0) & (k < taps), rolled, 0.0))
        tiles.append(jnp.concatenate(cols, axis=1) if len(cols) > 1 else cols[0])
    return jnp.concatenate(tiles, axis=0)


def as_column(row):
    count = row.shape[1]
    lane = lax.broadcasted_iota(jnp.int32, (count, count), 1)
    index = lax.broadcasted_iota(jnp.int32, (count, count), 0)
    return jnp.sum(jnp.where(lane == index, row, 0.0), axis=1, keepdims=True)


def sinc(x):
    angle = jnp.where(x == 0, 1.0, jnp.pi * x)
    return jnp.where(x == 0, 1.0, jnp.sin(angle) / angle)


def match_kernel(own_ref, x_ref, c_ref, rtap_ref, ctap_ref, sub_ref, *refs, strips, parts, visits):
    outs = refs[: strips * parts]
    rbig, s_win, h_win, powers, held, tap_rows, basis, table, shifts = refs[strips * parts :]
    filters, taps = rtap_ref.shape
    length = x_ref.shape[1]
    half = length // 2
    middle = taps // 2
    win = -(-(half + middle) // 16) * 16
    step = pl.program_id(0)

    @pl.when(step == 0)
    def _():
        tap_rows[...] = jnp.zeros(tap_rows.shape, jnp.float32)
        tap_rows[0:filters, 0:taps] = rtap_ref[...].astype(jnp.float32)
        tap_rows[8 : 8 + filters, 0:taps] = ctap_ref[...].astype(jnp.float32)
        i = lax.broadcasted_iota(jnp.int32, (LANES, LANES), 0)
        j = lax.broadcasted_iota(jnp.int32, (LANES, LANES), 1)
        flip = (i + j == taps - 1).astype(jnp.float32).astype(jnp.bfloat16)
        flipped = jnp.dot(
            tap_rows[0:8, :].astype(jnp.bfloat16), flip, preferred_element_type=jnp.float32
        )
        for b in range(filters):
            band = banded_rows(flipped[b : b + 1, :], length, taps, -middle)
            rbig[:, b * length : (b + 1) * length] = band.astype(jnp.bfloat16)
        s_win[...] = jnp.zeros(s_win.shape, jnp.bfloat16)
        h_win[...] = jnp.zeros(h_win.shape, jnp.bfloat16)
        powers[...] = jnp.zeros(powers.shape, jnp.float32)
        basis[...] = jnp.zeros(basis.shape, jnp.float32)
        for a in range(filters):
            row = jnp.broadcast_to(tap_rows[8 + a : 9 + a, :], (8, LANES))
            for b in range(filters):
                tile, off = divmod(b * SEG, LANES)
                moved = pltpu.roll(row, off, 1) if off else row
                basis[a * filters + b : a * filters + b + 1, tile * LANES : (tile + 1) * LANES] = (
                    moved[0:1]
                )
        lanes = lax.broadcasted_iota(jnp.int32, (1, LANES), 1).astype(jnp.float32)
        for axis, steps in enumerate((2.0 - lanes, lanes - 3.0)):
            distance = steps + as_column(sub_ref[axis : axis + 1, :])
            value = sinc(distance) * sinc(distance / 3.0)
            shifts[axis] = jnp.where(jnp.abs(distance) < 3.0, value, 0.0)
        count, terms = c_ref.shape[1:]
        for tile in range(basis.shape[1] // LANES):
            table[6 * tile : 6 * tile + 6] = jnp.dot(
                c_ref[...].reshape(6 * count, terms),
                basis[0:terms, tile * LANES : (tile + 1) * LANES],
                precision=lax.Precision.HIGHEST,
                preferred_element_type=jnp.float32,
            ).reshape(6, count, LANES)

    image = x_ref[0].astype(jnp.bfloat16)
    for b in range(filters):
        smooth = jnp.dot(
            image, rbig[:, b * length : (b + 1) * length], preferred_element_type=jnp.float32
        ).astype(jnp.bfloat16)
        s_win[0, b * win : (b + 1) * win, :] = smooth[0:win]
        s_win[1, b * win : (b + 1) * win, :] = smooth[length - win :]

    lane, diff = iotas(8)
    terms = [
        [
            jnp.broadcast_to(table[6 * tile + j, pl.ds(step, 1), :], (8, LANES))
            for j in range(6)
        ]
        for tile in range(basis.shape[1] // LANES)
    ]
    for side in range(2):
        origin = side * (length - win)
        for group in range(half // 16):
            halves = []
            for sub in range(2):
                start = 16 * group + 8 * sub
                row = lax.broadcasted_iota(jnp.int32, (8, LANES), 0) + (side * half + start)
                u = 2.0 * row.astype(jnp.float32) / (length - 1) - 1.0
                compact = {}
                for tile in range(basis.shape[1] // LANES):
                    t = terms[tile]
                    compact[0, tile] = t[0] + u * (t[1] + u * t[3])
                    compact[1, tile] = t[2] + u * t[4]
                    compact[2, tile] = t[5]
                acc = {}
                for b in range(filters):
                    lead = b * win + side * half + start - middle - origin
                    first = max(lead, b * win)
                    last = min(lead + 7 + taps - 1, (b + 1) * win - 1)
                    masks = {}
                    for tile in range(first // LANES, last // LANES + 1):
                        k = diff + (LANES * tile - lead)
                        mask = (k >= 0) & (k < taps)
                        if lead < b * win:
                            mask &= lane >= b * win - LANES * tile
                        if lead + 7 + taps > (b + 1) * win:
                            mask &= lane < (b + 1) * win - LANES * tile
                        masks[tile] = mask
                    source, off = divmod(b * SEG, LANES)
                    for q in range(3):
                        rolled = skew(compact[q, source], lead - off)
                        for tile, mask in masks.items():
                            acc[q, tile] = jnp.where(mask, rolled, acc.get((q, tile), 0.0))
                halves.append(acc)
            for q, tile in sorted(set(halves[0]) | set(halves[1])):
                zero = jnp.zeros((8, LANES), jnp.float32)
                both = jnp.concatenate([h.get((q, tile), zero) for h in halves], axis=0)
                h_win[
                    side,
                    q * half + 16 * group : q * half + 16 * group + 16,
                    tile * LANES : (tile + 1) * LANES,
                ] = both.astype(jnp.bfloat16)

    col = lax.broadcasted_iota(jnp.int32, (1, length), 1).astype(jnp.float32)
    w = 2.0 * col / (length - 1) - 1.0
    vertical = split(banded_rows(shifts[0, pl.ds(step, 1), :], half, 6, -2))
    horizontal = split(banded_rows(shifts[1, pl.ds(step, 1), :], half, 6, -3))
    left = jnp.concatenate([vertical[0], vertical[0], vertical[1]], axis=1)
    right = jnp.concatenate([horizontal[0], horizontal[0], horizontal[1]], axis=0)
    power = jnp.zeros((1, LANES), jnp.float32)
    for side in range(2):
        z = jnp.dot(h_win[side], s_win[side], preferred_element_type=jnp.float32)
        matched = z[0:half] + w * (z[half : 2 * half] + w * z[2 * half :])
        squares = jnp.sum(matched * matched, axis=0, keepdims=True)
        power += squares[:, :half] + squares[:, half:]
        high, low = split(matched)
        stacked = jnp.concatenate([high, low, high], axis=0)
        moved = jnp.dot(left, stacked, preferred_element_type=jnp.float32)
        for c in range(2):
            high, low = split(moved[:, c * half : (c + 1) * half])
            lhs = jnp.concatenate([high, low, high], axis=1)
            held[2 * side + c] = jnp.dot(lhs, right, preferred_element_type=jnp.float32)
    visit = pl.ds(step % visits, 1)
    powers[visit, :] = powers[visit, :] + power
    height = half // strips // parts
    for k in range(strips):
        for part in range(parts):
            begin = ((own_ref[0] ^ k) * parts + part) * height
            rows = pl.ds(pl.multiple_of(begin, height), height)
            out = outs[k * parts + part]
            for block in range(4):
                at = pl.ds(pl.multiple_of((4 * step + block) * height, height), height)
                out[at, :] = held[block, rows, :]

    @pl.when(step == pl.num_programs(0) - 1)
    def _():
        for k in range(strips):
            out = outs[k * parts]
            out[out.shape[0] - powers.shape[0] :, :] = powers[...]


def match_and_warp(own, images, coeffs, row_taps, col_taps, subpixel, strips, parts, visits):
    count, length, _ = images.shape
    filters, taps = row_taps.shape
    half = length // 2
    win = -(-(half + taps // 2) // 16) * 16
    depth = -(-filters * win // LANES) * LANES
    pow_rows = -(-visits // 8) * 8
    rows = count * 4 * half // strips // parts
    shapes = []
    for _ in range(strips):
        for part in range(parts):
            extra = pow_rows if part == 0 else 0
            shapes.append(jax.ShapeDtypeStruct((rows + extra, half), jnp.float32))
    return pl.pallas_call(
        functools.partial(match_kernel, strips=strips, parts=parts, visits=visits),
        grid_spec=pltpu.PrefetchScalarGridSpec(
            num_scalar_prefetch=1,
            grid=(count,),
            in_specs=[
                pl.BlockSpec((1, length, length), lambda i, own: (i, 0, 0)),
                pl.BlockSpec(coeffs.shape, lambda i, own: (0, 0, 0)),
                pl.BlockSpec(row_taps.shape, lambda i, own: (0, 0)),
                pl.BlockSpec(col_taps.shape, lambda i, own: (0, 0)),
                pl.BlockSpec(subpixel.shape, lambda i, own: (0, 0)),
            ],
            out_specs=[pl.BlockSpec(s.shape, lambda i, own: (0, 0)) for s in shapes],
            scratch_shapes=[
                pltpu.VMEM((length, filters * length), jnp.bfloat16),
                pltpu.VMEM((2, depth, length), jnp.bfloat16),
                pltpu.VMEM((2, 3 * half, depth), jnp.bfloat16),
                pltpu.VMEM((pow_rows, LANES), jnp.float32),
                pltpu.VMEM((4, half, half), jnp.float32),
                pltpu.VMEM((16, LANES), jnp.float32),
                pltpu.VMEM((-(-filters * filters // 8) * 8, -(-filters * SEG // LANES) * LANES), jnp.float32),
                pltpu.VMEM((6 * -(-filters * SEG // LANES), count, LANES), jnp.float32),
                pltpu.VMEM((2, count, LANES), jnp.float32),
            ],
        ),
        out_shape=shapes,
        name="match_and_warp",
    )(own, images, coeffs, row_taps, col_taps, subpixel)


def reduce_kernel(own_ref, dest_ref, slot_ref, *refs, strips, slots, images, visits, pixels):
    pieces = refs[:strips]
    others = refs[strips:-4]
    out_ref, var_ref, acc0, acc1 = refs[-4:]
    pow_rows = var_ref.shape[0]
    height = out_ref.shape[0] // slots
    total = others[0][...]
    for other in others[1:]:
        total = total + other[...]
    total = jnp.sum(total, axis=1, keepdims=True)
    variance = jnp.broadcast_to(total / pixels + 1e-05, (pow_rows, LANES))
    var_ref[...] = variance
    weight = 1.0 / variance
    acc0[...] = jnp.zeros(acc0.shape, jnp.float32)
    acc1[...] = jnp.zeros(acc1.shape, jnp.float32)
    own = own_ref[0]
    for image in range(images):
        visit = image % visits
        scale = jnp.broadcast_to(weight[visit : visit + 1], (height, LANES))
        for k in range(strips):
            for block in range(4):
                item = 4 * image + block
                acc = acc0 if block % 2 == 0 else acc1
                slot = dest_ref[own ^ k, item]
                at = pl.ds(pl.multiple_of(slot * height, height), height)
                rows = slice(item * height, (item + 1) * height)
                acc[at, :] = acc[at, :] + scale * pieces[k][rows, :]
    devices, items = slot_ref.shape
    lane = lax.broadcasted_iota(jnp.int32, (pow_rows, items), 1)
    row = lax.broadcasted_iota(jnp.int32, (pow_rows, items), 0)
    by_item = jnp.sum(
        jnp.where(lane // 4 % visits == row, weight[:, 0:1], 0.0), axis=0, keepdims=True
    )
    index = lax.broadcasted_iota(jnp.int32, (slots, items), 0)
    hits = jnp.zeros((slots, items), jnp.float32)
    for device in range(devices):
        hits = hits + jnp.where(slot_ref[device : device + 1, :] == index, 1.0, 0.0)
    denom = jnp.sum(hits * by_item, axis=1, keepdims=True)
    inverse = 1.0 / jnp.where(denom > 0, denom, 1.0)
    for slot in range(slots):
        at = slice(slot * height, (slot + 1) * height)
        scale = jnp.broadcast_to(inverse[slot : slot + 1, :], (height, LANES))
        out_ref[at, :] = (acc0[at, :] + acc1[at, :]) * scale


def reduce_blocks(own, dest, pieces, powers, slots, images, visits, pixels):
    pow_rows = powers[0].shape[0]
    height = pieces[0].shape[0] // (images * 4)
    smem = pl.BlockSpec(memory_space=pltpu.SMEM)
    vmem = pl.BlockSpec(memory_space=pltpu.VMEM)
    kernel = functools.partial(
        reduce_kernel,
        strips=len(pieces),
        slots=slots,
        images=images,
        visits=visits,
        pixels=pixels,
    )
    return pl.pallas_call(
        kernel,
        in_specs=[smem, smem] + [vmem] * (1 + len(pieces) + len(powers)),
        out_specs=[vmem, vmem],
        out_shape=[
            jax.ShapeDtypeStruct((slots * height, LANES), jnp.float32),
            jax.ShapeDtypeStruct((pow_rows, LANES), jnp.float32),
        ],
        scratch_shapes=[pltpu.VMEM((slots * height, LANES), jnp.float32)] * 2,
        name="reduce_blocks",
    )(own, dest, dest, *pieces, *powers)


def finish_kernel(own_ref, dest_ref, var_ref, *refs, visits, parts):
    warped = refs[: 2 * parts]
    templates = refs[2 * parts : 4 * parts]
    out_ref = refs[-1]
    own = own_ref[0]
    image_count = out_ref.shape[0]
    height = out_ref.shape[2] // 2 // parts
    inverse = 1.0 / jnp.sqrt(var_ref[...])
    for image in range(image_count):
        visit = image % visits
        scale = jnp.broadcast_to(inverse[visit : visit + 1, :], (height, LANES))
        for block in range(4):
            item = 4 * image + block
            slot = dest_ref[own, item]
            at = pl.ds(pl.multiple_of(slot * height, height), height)
            for k in range(2):
                for part in range(parts):
                    here = warped[k * parts + part][item * height : (item + 1) * height, :]
                    template = templates[k * parts + part][at, :]
                    begin = (((own & 1) ^ k) * parts + part) * height
                    rows = pl.ds(pl.multiple_of(begin, height), height)
                    out_ref[image, block, rows, :] = (here - template) * scale


def finish(own, dest, variance, warped, templates, previous, pair, strips, images, visits, parts):
    height = warped[1].shape[0] // (images * 4)
    side = height * parts * strips
    smem = pl.BlockSpec(memory_space=pltpu.SMEM)

    def whole(x):
        return pl.BlockSpec(x.shape, lambda i, own: (0, 0))

    extra = [] if previous is None else [previous]
    inputs = [variance, *warped, *templates]
    return pl.pallas_call(
        functools.partial(finish_kernel, visits=visits, parts=parts),
        grid_spec=pltpu.PrefetchScalarGridSpec(
            num_scalar_prefetch=1,
            grid=(1,),
            in_specs=[smem]
            + [whole(x) for x in inputs]
            + [pl.BlockSpec(memory_space=pl.ANY) for _ in extra],
            out_specs=pl.BlockSpec(
                (images, 4, 2 * height * parts, LANES),
                lambda i, own: (0, 0, (own[0] % strips // 2) ^ (pair // 2), 0),
            ),
        ),
        out_shape=jax.ShapeDtypeStruct((images, 4, side, LANES), jnp.float32),
        input_output_aliases={2 + len(inputs): 0} if extra else {},
        name="finish",
    )(own, dest, *inputs, *extra)


GROUP = 8
PARTS = 2


def per_device(exposures, row_taps, col_taps, kernel_coeffs, subpixel, destination):
    tile_count, visits, length = exposures.shape[:3]
    filters, _ = row_taps.shape
    devices = lax.axis_size("tile")
    own = lax.axis_index("tile").astype(jnp.int32).reshape(1)
    images = tile_count * visits
    slots = tile_count * devices * 4
    pixels = tile_count * devices * length * length
    dest = destination.reshape(devices, images * 4)

    def permute(x, target):
        return lax.ppermute(x, "tile", [(i, target(i)) for i in range(devices)])

    def swap(x, k):
        return permute(x, lambda i: i ^ k)

    def ahead(x, groups):
        return permute(x, lambda i: (i + groups * GROUP) % devices)

    warped = match_and_warp(
        own % GROUP,
        exposures.reshape(images, length, length),
        kernel_coeffs.transpose(3, 0, 1, 2).reshape(-1, images, filters * filters),
        row_taps,
        col_taps,
        subpixel.transpose(2, 0, 1).reshape(2, images),
        GROUP,
        PARTS,
        visits,
    )
    others = devices // GROUP
    pow_rows = -(-visits // 8) * 8
    full = []
    pieces = []
    for part in range(PARTS):
        mine = [warped[k * PARTS + part] for k in range(GROUP)]
        pieces.append([mine[0]] + [swap(mine[k], k) for k in range(1, GROUP)])
    power = pieces[0][0][-pow_rows:]
    for piece in pieces[0][1:]:
        power = power + piece[-pow_rows:]
    powers = [power] + [ahead(power, r) for r in range(1, others)]
    for part in range(PARTS):
        partial, variance = reduce_blocks(
            own, dest, pieces[part], powers, slots, images, visits, pixels
        )
        moved = [ahead(partial, r) for r in range(1, others)]
        template = partial
        for piece in moved:
            template = template + piece
        two = swap(template, 2)
        four = swap(template, 4)
        six = swap(two, 4) if part == 0 else swap(four, 2)
        full.append(
            [template, swap(template, 1)]
            + [two, swap(two, 1)]
            + [four, swap(four, 1)]
            + [six, swap(six, 1)]
        )
    result = None
    for pair in range(0, GROUP, 2):
        keys = [(k, part) for k in (pair, pair + 1) for part in range(PARTS)]
        result = finish(
            own,
            dest,
            variance,
            [warped[k * PARTS + part] for k, part in keys],
            [full[part][k] for k, part in keys],
            result,
            pair,
            GROUP,
            images,
            visits,
            PARTS,
        )
    return result.reshape(tile_count, visits, 4, BLOCK, BLOCK)


def solution(mesh):
    return jax.shard_map(
        per_device,
        mesh=mesh,
        in_specs=(
            P(("groups", "tile"), None, None, None),
            P(),
            P(),
            P(("groups", "tile"), None, None, None),
            P(("groups", "tile"), None, None),
            P("groups", None),
        ),
        out_specs=P(("groups", "tile"), None, None, None, None),
        check_vma=False,
    )
```

profile of v0, /device:TPU:0, one launch (start us, length us, event | category | flops | bytes accessed | tf_op | source)
XLA Modules:
  0.0 111.1 jit_solution(12064884683645181305)
XLA Ops:
  0.0 17.6 %match_and_warp.1 = (f32[264,128]{1,0:T(8,128)}, f32[256,128]{1,0:T(8,128)}, f32[264,128]{1,0:T(8,128)}, f32[256,128]{1,0:T(8,128)}, f32[264,128]{1,0:T(8,128)},...) custom-call(s32[1]{0:T(128)S(6)} %select_n.7.own_ref, ...), custom_call_target="tpu_custom_call" | custom-call | tf_op jit(solution)/shard_map/match_and_warp/pallas_call | solution.py:221
  17.6 3.1 %collective-permute-start.10 = (f32[264,128]{1,0:T(8,128)}, f32[264,128]{1,0:T(8,128)S(1)}, u32[]{:S(2)}, u32[]{:S(2)}) collective-permute-start(f32[264,128]{1,0:T(8,128)} %get-tuple-element.36.refs_0_), channel_id=1, source_target_pairs={{0,4},{1,5},{2,6},{3,7},{4,0},{5,1},{6,2},{7,3},{8,12},{9,13},{10,... | collective-permute-start | bytes 405512 | tf_op jit(solution)/shard_map/ppermute | solution.py:390
  20.7 0.2 collective-permute-start
  20.9 1.9 %collective-permute-start.1 = (f32[256,128]{1,0:T(8,128)}, f32[256,128]{1,0:T(8,128)S(1)}, u32[]{:S(2)}, u32[]{:S(2)}) collective-permute-start(f32[256,128]{1,0:T(8,128)} %get-tuple-element.26.refs_1_), channel_id=1, source_target_pairs={{0,2},{1,3},{2,0},{3,1},{4,6},{5,7},{6,4},{7,5},{8,10},{9,11},{10,... | collective-permute-start | bytes 393224 | tf_op jit(solution)/shard_map/ppermute | solution.py:390
  22.8 1.5 %collective-permute-start.12 = (f32[264,128]{1,0:T(8,128)}, f32[264,128]{1,0:T(8,128)S(1)}, u32[]{:S(2)}, u32[]{:S(2)}) collective-permute-start(f32[264,128]{1,0:T(8,128)} %get-tuple-element.38.refs_0_), channel_id=1, source_target_pairs={{0,6},{1,7},{2,4},{3,5},{4,2},{5,3},{6,0},{7,1},{8,14},{9,15},{10,... | collective-permute-start | bytes 405512 | tf_op jit(solution)/shard_map/ppermute | solution.py:390
  24.3 0.7 collective-permute-start.13
  25.0 1.9 %collective-permute-done.1.refs_2_ = f32[256,128]{1,0:T(8,128)S(1)} collective-permute-done((f32[256,128]{1,0:T(8,128)}, f32[256,128]{1,0:T(8,128)S(1)}, u32[]{:S(2)}, u32[]{:S(2)}) %collective-permute-start.1) | collective-permute-done | bytes 131104 | tf_op jit(solution)/shard_map/ppermute | solution.py:390
  26.9 1.8 %collective-permute-start.8 = (f32[264,128]{1,0:T(8,128)}, f32[264,128]{1,0:T(8,128)S(1)}, u32[]{:S(2)}, u32[]{:S(2)}) collective-permute-start(f32[264,128]{1,0:T(8,128)} %get-tuple-element.34.refs_0_), channel_id=1, source_target_pairs={{0,2},{1,3},{2,0},{3,1},{4,6},{5,7},{6,4},{7,5},{8,10},{9,11},{10,... | collective-permute-start | bytes 405512 | tf_op jit(solution)/shard_map/ppermute | solution.py:390
  28.7 0.9 collective-permute-start.9
  29.6 2.7 %collective-permute-done.12.refs_6_ = f32[264,128]{1,0:T(8,128)S(1)} collective-permute-done((f32[264,128]{1,0:T(8,128)}, f32[264,128]{1,0:T(8,128)S(1)}, u32[]{:S(2)}, u32[]{:S(2)}) %collective-permute-start.12) | collective-permute-done | bytes 135200 | tf_op jit(solution)/shard_map/ppermute | solution.py:390
  32.3 1.4 %collective-permute-done.13.refs_7_ = f32[264,128]{1,0:T(8,128)S(1)} collective-permute-done((f32[264,128]{1,0:T(8,128)}, f32[264,128]{1,0:T(8,128)S(1)}, u32[]{:S(2)}, u32[]{:S(2)}) %collective-permute-start.13) | collective-permute-done | bytes 135200 | tf_op jit(solution)/shard_map/ppermute | solution.py:390
  33.7 1.2 %collective-permute-start.3 = (f32[256,128]{1,0:T(8,128)}, f32[256,128]{1,0:T(8,128)S(1)}, u32[]{:S(2)}, u32[]{:S(2)}) collective-permute-start(f32[256,128]{1,0:T(8,128)} %get-tuple-element.28.refs_1_), channel_id=1, source_target_pairs={{0,4},{1,5},{2,6},{3,7},{4,0},{5,1},{6,2},{7,3},{8,12},{9,13},{10,... | collective-permute-start | bytes 393224 | tf_op jit(solution)/shard_map/ppermute | solution.py:390
  34.9 0.7 collective-permute-start.4
  35.6 1.7 %collective-permute-done.8.refs_2_ = f32[264,128]{1,0:T(8,128)S(1)} collective-permute-done((f32[264,128]{1,0:T(8,128)}, f32[264,128]{1,0:T(8,128)S(1)}, u32[]{:S(2)}, u32[]{:S(2)}) %collective-permute-start.8) | collective-permute-done | bytes 135200 | tf_op jit(solution)/shard_map/ppermute | solution.py:390
  37.3 1.5 %collective-permute-start.5 = (f32[256,128]{1,0:T(8,128)}, f32[256,128]{1,0:T(8,128)S(1)}, u32[]{:S(2)}, u32[]{:S(2)}) collective-permute-start(f32[256,128]{1,0:T(8,128)} %get-tuple-element.30.refs_1_), channel_id=1, source_target_pairs={{0,6},{1,7},{2,4},{3,5},{4,2},{5,3},{6,0},{7,1},{8,14},{9,15},{10,... | collective-permute-start | bytes 393224 | tf_op jit(solution)/shard_map/ppermute | solution.py:390
  38.8 1.3 %collective-permute-done.9.refs_3_ = f32[264,128]{1,0:T(8,128)S(1)} collective-permute-done((f32[264,128]{1,0:T(8,128)}, f32[264,128]{1,0:T(8,128)S(1)}, u32[]{:S(2)}, u32[]{:S(2)}) %collective-permute-start.9) | collective-permute-done | bytes 135200 | tf_op jit(solution)/shard_map/ppermute | solution.py:390
  40.1 1.3 %collective-permute-start.6 = (f32[256,128]{1,0:T(8,128)}, f32[256,128]{1,0:T(8,128)S(1)}, u32[]{:S(2)}, u32[]{:S(2)}) collective-permute-start(f32[256,128]{1,0:T(8,128)} %get-tuple-element.31.refs_3_), channel_id=1, source_target_pairs={{0,7},{1,6},{2,5},{3,4},{4,3},{5,2},{6,1},{7,0},{8,15},{9,14},{10,... | collective-permute-start | bytes 393224 | tf_op jit(solution)/shard_map/ppermute | solution.py:390
  41.4 0.7 slice_add_fusion.refs_8_
  42.1 6.4 %collective-permute-done.2.refs_3_ = f32[256,128]{1,0:T(8,128)S(1)} collective-permute-done((f32[256,128]{1,0:T(8,128)}, f32[256,128]{1,0:T(8,128)S(1)}, u32[]{:S(2)}, u32[]{:S(2)}) %collective-permute-start.2) | collective-permute-done | bytes 131104 | tf_op jit(solution)/shard_map/ppermute | solution.py:390
  48.5 2.6 %collective-permute-start.14 = (f32[8,128]{1,0:T(8,128)S(1)}, f32[8,128]{1,0:T(8,128)S(1)}, u32[]{:S(2)}, u32[]{:S(2)}) collective-permute-start(f32[8,128]{1,0:T(8,128)S(1)} %slice_add_fusion.refs_8_), channel_id=1, source_target_pairs={{0,8},{1,9},{2,10},{3,11},{4,12},{5,13},{6,14},{7,15},{8,0},{9,1},... | collective-permute-start | bytes 12296 | tf_op jit(solution)/shard_map/ppermute | solution.py:390
  51.2 1.9 %collective-permute-done.14.refs_9_ = f32[8,128]{1,0:T(8,128)S(1)} collective-permute-done((f32[8,128]{1,0:T(8,128)S(1)}, f32[8,128]{1,0:T(8,128)S(1)}, u32[]{:S(2)}, u32[]{:S(2)}) %collective-permute-start.14) | collective-permute-done | bytes 4128 | tf_op jit(solution)/shard_map/ppermute | solution.py:390
  53.1 0.5 copy-done.28
  53.6 2.8 %reduce_blocks.2 = (f32[512,128]{1,0:T(8,128)}, f32[8,128]{1,0:T(8,128)}) custom-call(s32[1]{0:T(128)} %bitcast.own_ref, s32[16,32]{1,0:T(8,128)} %dest_ref.11, s32[16,32]{1,0:T(8,128)} %dest_ref.11, f32[256,128]{1,0:T(8,128)} %get-tuple-element.24.refs_0_.refs_1_, f32[256,128]{1,0:T(8,128)} %copy-done.20, f32[256,128]{1,0:T(8,128)} %copy-done.21, ...), custom_call_target="tpu_custom_call" | custom-call | tf_op jit(solution)/shard_map/reduce_blocks/pallas_call | solution.py:309
  56.4 2.6 %collective-permute-start.18 = (f32[512,128]{1,0:T(8,128)}, f32[512,128]{1,0:T(8,128)S(1)}, u32[]{:S(2)}, u32[]{:S(2)}) collective-permute-start(f32[512,128]{1,0:T(8,128)} %get-tuple-element.42), channel_id=1, source_target_pairs={{0,8},{1,9},{2,10},{3,11},{4,12},{5,13},{6,14},{7,15},{8,0},{9,1},... | collective-permute-start | bytes 786440 | tf_op jit(solution)/shard_map/ppermute | solution.py:390
  59.0 2.8 %reduce_blocks.3 = (f32[512,128]{1,0:T(8,128)}, f32[8,128]{1,0:T(8,128)}) custom-call(s32[1]{0:T(128)} %bitcast.own_ref, s32[16,32]{1,0:T(8,128)} %dest_ref.11, s32[16,32]{1,0:T(8,128)} %dest_ref.11, f32[264,128]{1,0:T(8,128)} %get-tuple-element.32.refs_0_, f32[264,128]{1,0:T(8,128)} %copy-done.17, f32[264,128]{1,0:T(8,128)} %copy-done.18, ...), custom_call_target="tpu_custom_call" | custom-call | tf_op jit(solution)/shard_map/reduce_blocks/pallas_call | solution.py:309
  61.8 0.3 collective-permute-start.15
  62.2 14.9 %collective-permute-done.18 = f32[512,128]{1,0:T(8,128)S(1)} collective-permute-done((f32[512,128]{1,0:T(8,128)}, f32[512,128]{1,0:T(8,128)S(1)}, u32[]{:S(2)}, u32[]{:S(2)}) %collective-permute-start.18) | collective-permute-done | bytes 262176 | tf_op jit(solution)/shard_map/ppermute | solution.py:390
  77.0 1.0 add.42.refs_5_
  78.0 0.1 collective-permute-start.30
  78.2 0.1 collective-permute-start.19
  78.3 3.3 %collective-permute-done.15 = f32[512,128]{1,0:T(8,128)S(1)} collective-permute-done((f32[512,128]{1,0:T(8,128)}, f32[512,128]{1,0:T(8,128)S(1)}, u32[]{:S(2)}, u32[]{:S(2)}) %collective-permute-start.15) | collective-permute-done | bytes 262176 | tf_op jit(solution)/shard_map/ppermute | solution.py:390
  81.5 1.0 add.41.refs_4_
  82.6 0.1 collective-permute-start.29
  82.7 0.8 collective-permute-start.23
  83.5 3.8 %collective-permute-done.26.refs_5_ = f32[512,128]{1,0:T(8,128)S(1)} collective-permute-done((f32[512,128]{1,0:T(8,128)S(1)}, f32[512,128]{1,0:T(8,128)S(1)}, u32[]{:S(2)}, u32[]{:S(2)}) %collective-permute-start.26) | collective-permute-done | bytes 262176 | tf_op jit(solution)/shard_map/ppermute | solution.py:390
  87.4 2.0 %collective-permute-start.20 = (f32[512,128]{1,0:T(8,128)S(1)}, f32[512,128]{1,0:T(8,128)S(1)}, u32[]{:S(2)}, u32[]{:S(2)}) collective-permute-start(f32[512,128]{1,0:T(8,128)S(1)} %collective-permute-done.19.refs_5_), channel_id=1, source_target_pairs={{0,2},{1,3},{2,0},{3,1},{4,6},{5,7},{6,4},{7,5},{8,10},{9,11},{10,... | collective-permute-start | bytes 786440 | tf_op jit(solution)/shard_map/ppermute | solution.py:390
  89.4 3.6 %collective-permute-done.16.refs_4_ = f32[512,128]{1,0:T(8,128)S(1)} collective-permute-done((f32[512,128]{1,0:T(8,128)S(1)}, f32[512,128]{1,0:T(8,128)S(1)}, u32[]{:S(2)}, u32[]{:S(2)}) %collective-permute-start.16) | collective-permute-done | bytes 262176 | tf_op jit(solution)/shard_map/ppermute | solution.py:390
  93.0 0.1 collective-permute-start.27
  93.1 0.5 collective-permute-start.25
  93.6 0.1 collective-permute-start.24
  93.7 4.4 %collective-permute-done.20.refs_5_ = f32[512,128]{1,0:T(8,128)S(1)} collective-permute-done((f32[512,128]{1,0:T(8,128)S(1)}, f32[512,128]{1,0:T(8,128)S(1)}, u32[]{:S(2)}, u32[]{:S(2)}) %collective-permute-start.20) | collective-permute-done | bytes 262176 | tf_op jit(solution)/shard_map/ppermute | solution.py:390
  98.1 2.2 %collective-permute-done.17.refs_4_ = f32[512,128]{1,0:T(8,128)S(1)} collective-permute-done((f32[512,128]{1,0:T(8,128)S(1)}, f32[512,128]{1,0:T(8,128)S(1)}, u32[]{:S(2)}, u32[]{:S(2)}) %collective-permute-start.17) | collective-permute-done | bytes 262176 | tf_op jit(solution)/shard_map/ppermute | solution.py:390
  100.3 2.4 %finish.4.refs_8_ = f32[8,4,128,128]{3,2,1,0:T(8,128)} custom-call(s32[1]{0:T(128)} %bitcast.own_ref, s32[16,32]{1,0:T(8,128)} %dest_ref.11, f32[8,128]{1,0:T(8,128)} %get-tuple-element.40.var_ref, f32[264,128]{1,0:T(8,128)} %get-tuple-element.32.refs_0_, f32[256,128]{1,0:T(8,128)} %get-tuple-element.24.refs_0_.refs_1_, ...), custom_call_target="tpu_custom_call" | custom-call | tf_op jit(solution)/shard_map/finish/pallas_call | solution.py:356
  102.7 2.3 %finish.5.refs_8_ = f32[8,4,128,128]{3,2,1,0:T(8,128)} custom-call(s32[1]{0:T(128)} %bitcast.own_ref, s32[16,32]{1,0:T(8,128)} %dest_ref.11, f32[8,128]{1,0:T(8,128)} %get-tuple-element.40.var_ref, f32[264,128]{1,0:T(8,128)} %get-tuple-element.34.refs_0_, f32[256,128]{1,0:T(8,128)} %get-tuple-element.26.refs_1_, ...), custom_call_target="tpu_custom_call", output_to_operand_aliasing={{}: (11, {})} | custom-call | tf_op jit(solution)/shard_map/finish/pallas_call | solution.py:356
  105.1 0.7 copy-done.12
  105.7 2.3 %finish.6.refs_8_ = f32[8,4,128,128]{3,2,1,0:T(8,128)} custom-call(s32[1]{0:T(128)} %bitcast.own_ref, s32[16,32]{1,0:T(8,128)} %dest_ref.11, f32[8,128]{1,0:T(8,128)} %get-tuple-element.40.var_ref, f32[264,128]{1,0:T(8,128)} %get-tuple-element.36.refs_0_, f32[256,128]{1,0:T(8,128)} %get-tuple-element.28.refs_1_, ...), custom_call_target="tpu_custom_call", output_to_operand_aliasing={{}: (11, {})} | custom-call | tf_op jit(solution)/shard_map/finish/pallas_call | solution.py:356
  108.1 0.7 copy-done.11
  108.8 2.3 %finish.7 = f32[8,4,128,128]{3,2,1,0:T(8,128)} custom-call(s32[1]{0:T(128)} %bitcast.own_ref, s32[16,32]{1,0:T(8,128)} %dest_ref.11, f32[8,128]{1,0:T(8,128)} %get-tuple-element.40.var_ref, f32[264,128]{1,0:T(8,128)} %get-tuple-element.38.refs_0_, f32[256,128]{1,0:T(8,128)} %get-tuple-element.30.refs_1_, ...), custom_call_target="tpu_custom_call", output_to_operand_aliasing={{}: (11, {})} | custom-call | tf_op jit(solution)/shard_map/finish/pallas_call | solution.py:356
  (82 shorter events, 0.4 us)
Async XLA Ops:
  17.6 9.2 %collective-permute-start.10 = (f32[264,128]{1,0:T(8,128)}, f32[264,128]{1,0:T(8,128)S(1)}, u32[]{:S(2)}, u32[]{:S(2)}) collective-permute-start(f32[264,128]{1,0:T(8,128)} %get-tuple-element.36.refs_0_), channel_id=1, source_target_pairs={{0,4},{1,5},{2,6},{3,7},{4,0},{5,1},{6,2},{7,3},{8,12},{9,13},{10,... | collective-permute-start | bytes 405512 | tf_op jit(solution)/shard_map/ppermute | solution.py:390
  20.7 7.9 %collective-permute-start.11 = (f32[264,128]{1,0:T(8,128)}, f32[264,128]{1,0:T(8,128)S(1)}, u32[]{:S(2)}, u32[]{:S(2)}) collective-permute-start(f32[264,128]{1,0:T(8,128)} %get-tuple-element.37.refs_2_), channel_id=1, source_target_pairs={{0,5},{1,4},{2,7},{3,6},{4,1},{5,0},{6,3},{7,2},{8,13},{9,12},{10,... | collective-permute-start | bytes 405512 | tf_op jit(solution)/shard_map/ppermute | solution.py:390
  20.7 3.6 %collective-permute-start = (f32[256,128]{1,0:T(8,128)}, f32[256,128]{1,0:T(8,128)S(1)}, u32[]{:S(2)}, u32[]{:S(2)}) collective-permute-start(f32[256,128]{1,0:T(8,128)} %get-tuple-element.25.refs_3_), channel_id=1, source_target_pairs={{0,1},{1,0},{2,3},{3,2},{4,5},{5,4},{6,7},{7,6},{8,9},{9,8},{10,11... | collective-permute-start | bytes 393224 | tf_op jit(solution)/shard_map/ppermute | solution.py:390
  20.9 5.9 %collective-permute-start.1 = (f32[256,128]{1,0:T(8,128)}, f32[256,128]{1,0:T(8,128)S(1)}, u32[]{:S(2)}, u32[]{:S(2)}) collective-permute-start(f32[256,128]{1,0:T(8,128)} %get-tuple-element.26.refs_1_), channel_id=1, source_target_pairs={{0,2},{1,3},{2,0},{3,1},{4,6},{5,7},{6,4},{7,5},{8,10},{9,11},{10,... | collective-permute-start | bytes 393224 | tf_op jit(solution)/shard_map/ppermute | solution.py:390
  22.8 9.5 %collective-permute-start.12 = (f32[264,128]{1,0:T(8,128)}, f32[264,128]{1,0:T(8,128)S(1)}, u32[]{:S(2)}, u32[]{:S(2)}) collective-permute-start(f32[264,128]{1,0:T(8,128)} %get-tuple-element.38.refs_0_), channel_id=1, source_target_pairs={{0,6},{1,7},{2,4},{3,5},{4,2},{5,3},{6,0},{7,1},{8,14},{9,15},{10,... | collective-permute-start | bytes 405512 | tf_op jit(solution)/shard_map/ppermute | solution.py:390
  24.3 28.7 %copy-start.20 = (f32[256,128]{1,0:T(8,128)}, f32[256,128]{1,0:T(8,128)S(1)}, u32[]{:S(2)}) copy-start(f32[256,128]{1,0:T(8,128)S(1)} %collective-permute-done.refs_1_) | copy-start | bytes 393220
  24.3 9.3 %collective-permute-start.13 = (f32[264,128]{1,0:T(8,128)}, f32[264,128]{1,0:T(8,128)S(1)}, u32[]{:S(2)}, u32[]{:S(2)}) collective-permute-start(f32[264,128]{1,0:T(8,128)} %get-tuple-element.39.refs_2_), channel_id=1, source_target_pairs={{0,7},{1,6},{2,5},{3,4},{4,3},{5,2},{6,1},{7,0},{8,15},{9,14},{10,... | collective-permute-start | bytes 405512 | tf_op jit(solution)/shard_map/ppermute | solution.py:390
  26.9 26.2 %copy-start.21 = (f32[256,128]{1,0:T(8,128)}, f32[256,128]{1,0:T(8,128)S(1)}, u32[]{:S(2)}) copy-start(f32[256,128]{1,0:T(8,128)S(1)} %collective-permute-done.1.refs_2_) | copy-start | bytes 393220
  26.9 8.0 %collective-permute-start.7 = (f32[264,128]{1,0:T(8,128)}, f32[264,128]{1,0:T(8,128)S(1)}, u32[]{:S(2)}, u32[]{:S(2)}) collective-permute-start(f32[264,128]{1,0:T(8,128)} %get-tuple-element.33.refs_2_), channel_id=1, source_target_pairs={{0,1},{1,0},{2,3},{3,2},{4,5},{5,4},{6,7},{7,6},{8,9},{9,8},{10,11... | collective-permute-start | bytes 405512 | tf_op jit(solution)/shard_map/ppermute | solution.py:390
  26.9 32.1 %copy-start.13 = (f32[264,128]{1,0:T(8,128)}, f32[264,128]{1,0:T(8,128)S(1)}, u32[]{:S(2)}) copy-start(f32[264,128]{1,0:T(8,128)S(1)} %collective-permute-done.10.refs_4_) | copy-start | bytes 405508
  26.9 10.4 %collective-permute-start.8 = (f32[264,128]{1,0:T(8,128)}, f32[264,128]{1,0:T(8,128)S(1)}, u32[]{:S(2)}, u32[]{:S(2)}) collective-permute-start(f32[264,128]{1,0:T(8,128)} %get-tuple-element.34.refs_0_), channel_id=1, source_target_pairs={{0,2},{1,3},{2,0},{3,1},{4,6},{5,7},{6,4},{7,5},{8,10},{9,11},{10,... | collective-permute-start | bytes 405512 | tf_op jit(solution)/shard_map/ppermute | solution.py:390
  28.6 30.3 %copy-start.14 = (f32[264,128]{1,0:T(8,128)}, f32[264,128]{1,0:T(8,128)S(1)}, u32[]{:S(2)}) copy-start(f32[264,128]{1,0:T(8,128)S(1)} %collective-permute-done.11.refs_5_) | copy-start | bytes 405508
  28.7 11.4 %collective-permute-start.9 = (f32[264,128]{1,0:T(8,128)}, f32[264,128]{1,0:T(8,128)S(1)}, u32[]{:S(2)}, u32[]{:S(2)}) collective-permute-start(f32[264,128]{1,0:T(8,128)} %get-tuple-element.35.refs_2_), channel_id=1, source_target_pairs={{0,3},{1,2},{2,1},{3,0},{4,7},{5,6},{6,5},{7,4},{8,11},{9,10},{10,... | collective-permute-start | bytes 405512 | tf_op jit(solution)/shard_map/ppermute | solution.py:390
  32.3 26.7 %copy-start.15 = (f32[264,128]{1,0:T(8,128)}, f32[264,128]{1,0:T(8,128)S(1)}, u32[]{:S(2)}) copy-start(f32[264,128]{1,0:T(8,128)S(1)} %collective-permute-done.12.refs_6_) | copy-start | bytes 405508
  32.3 16.2 %collective-permute-start.2 = (f32[256,128]{1,0:T(8,128)}, f32[256,128]{1,0:T(8,128)S(1)}, u32[]{:S(2)}, u32[]{:S(2)}) collective-permute-start(f32[256,128]{1,0:T(8,128)} %get-tuple-element.27.refs_3_), channel_id=1, source_target_pairs={{0,3},{1,2},{2,1},{3,0},{4,7},{5,6},{6,5},{7,4},{8,11},{9,10},{10,... | collective-permute-start | bytes 393224 | tf_op jit(solution)/shard_map/ppermute | solution.py:390
  33.7 25.3 %copy-start.16 = (f32[264,128]{1,0:T(8,128)}, f32[264,128]{1,0:T(8,128)S(1)}, u32[]{:S(2)}) copy-start(f32[264,128]{1,0:T(8,128)S(1)} %collective-permute-done.13.refs_7_) | copy-start | bytes 405508
  33.7 17.4 %collective-permute-start.3 = (f32[256,128]{1,0:T(8,128)}, f32[256,128]{1,0:T(8,128)S(1)}, u32[]{:S(2)}, u32[]{:S(2)}) collective-permute-start(f32[256,128]{1,0:T(8,128)} %get-tuple-element.28.refs_1_), channel_id=1, source_target_pairs={{0,4},{1,5},{2,6},{3,7},{4,0},{5,1},{6,2},{7,3},{8,12},{9,13},{10,... | collective-permute-start | bytes 393224 | tf_op jit(solution)/shard_map/ppermute | solution.py:390
  34.9 24.1 %copy-start.17 = (f32[264,128]{1,0:T(8,128)}, f32[264,128]{1,0:T(8,128)S(1)}, u32[]{:S(2)}) copy-start(f32[264,128]{1,0:T(8,128)S(1)} %collective-permute-done.7.refs_1_) | copy-start | bytes 405508
  34.9 16.2 %collective-permute-start.4 = (f32[256,128]{1,0:T(8,128)}, f32[256,128]{1,0:T(8,128)S(1)}, u32[]{:S(2)}, u32[]{:S(2)}) collective-permute-start(f32[256,128]{1,0:T(8,128)} %get-tuple-element.29.refs_3_), channel_id=1, source_target_pairs={{0,5},{1,4},{2,7},{3,6},{4,1},{5,0},{6,3},{7,2},{8,13},{9,12},{10,... | collective-permute-start | bytes 393224 | tf_op jit(solution)/shard_map/ppermute | solution.py:390
  37.3 21.7 %copy-start.18 = (f32[264,128]{1,0:T(8,128)}, f32[264,128]{1,0:T(8,128)S(1)}, u32[]{:S(2)}) copy-start(f32[264,128]{1,0:T(8,128)S(1)} %collective-permute-done.8.refs_2_) | copy-start | bytes 405508
  37.3 13.8 %collective-permute-start.5 = (f32[256,128]{1,0:T(8,128)}, f32[256,128]{1,0:T(8,128)S(1)}, u32[]{:S(2)}, u32[]{:S(2)}) collective-permute-start(f32[256,128]{1,0:T(8,128)} %get-tuple-element.30.refs_1_), channel_id=1, source_target_pairs={{0,6},{1,7},{2,4},{3,5},{4,2},{5,3},{6,0},{7,1},{8,14},{9,15},{10,... | collective-permute-start | bytes 393224 | tf_op jit(solution)/shard_map/ppermute | solution.py:390
  40.1 18.9 %copy-start.19 = (f32[264,128]{1,0:T(8,128)}, f32[264,128]{1,0:T(8,128)S(1)}, u32[]{:S(2)}) copy-start(f32[264,128]{1,0:T(8,128)S(1)} %collective-permute-done.9.refs_3_) | copy-start | bytes 405508
  40.1 11.1 %collective-permute-start.6 = (f32[256,128]{1,0:T(8,128)}, f32[256,128]{1,0:T(8,128)S(1)}, u32[]{:S(2)}, u32[]{:S(2)}) collective-permute-start(f32[256,128]{1,0:T(8,128)} %get-tuple-element.31.refs_3_), channel_id=1, source_target_pairs={{0,7},{1,6},{2,5},{3,4},{4,3},{5,2},{6,1},{7,0},{8,15},{9,14},{10,... | collective-permute-start | bytes 393224 | tf_op jit(solution)/shard_map/ppermute | solution.py:390
  42.1 10.9 %copy-start.27 = (f32[8,128]{1,0:T(8,128)}, f32[8,128]{1,0:T(8,128)S(1)}, u32[]{:S(2)}) copy-start(f32[8,128]{1,0:T(8,128)S(1)} %slice_add_fusion.refs_8_) | copy-start | bytes 12292
  48.5 4.5 %collective-permute-start.14 = (f32[8,128]{1,0:T(8,128)S(1)}, f32[8,128]{1,0:T(8,128)S(1)}, u32[]{:S(2)}, u32[]{:S(2)}) collective-permute-start(f32[8,128]{1,0:T(8,128)S(1)} %slice_add_fusion.refs_8_), channel_id=1, source_target_pairs={{0,8},{1,9},{2,10},{3,11},{4,12},{5,13},{6,14},{7,15},{8,0},{9,1},... | collective-permute-start | bytes 12296 | tf_op jit(solution)/shard_map/ppermute | solution.py:390
  56.4 20.7 %collective-permute-start.18 = (f32[512,128]{1,0:T(8,128)}, f32[512,128]{1,0:T(8,128)S(1)}, u32[]{:S(2)}, u32[]{:S(2)}) collective-permute-start(f32[512,128]{1,0:T(8,128)} %get-tuple-element.42), channel_id=1, source_target_pairs={{0,8},{1,9},{2,10},{3,11},{4,12},{5,13},{6,14},{7,15},{8,0},{9,1},... | collective-permute-start | bytes 786440 | tf_op jit(solution)/shard_map/ppermute | solution.py:390
  61.8 19.7 %collective-permute-start.15 = (f32[512,128]{1,0:T(8,128)}, f32[512,128]{1,0:T(8,128)S(1)}, u32[]{:S(2)}, u32[]{:S(2)}) collective-permute-start(f32[512,128]{1,0:T(8,128)} %get-tuple-element.41), channel_id=1, source_target_pairs={{0,8},{1,9},{2,10},{3,11},{4,12},{5,13},{6,14},{7,15},{8,0},{9,1},... | collective-permute-start | bytes 786440 | tf_op jit(solution)/shard_map/ppermute | solution.py:390
  78.0 22.2 %copy-start = (f32[512,128]{1,0:T(8,128)}, f32[512,128]{1,0:T(8,128)S(1)}, u32[]{:S(2)}) copy-start(f32[512,128]{1,0:T(8,128)S(1)} %add.42.refs_5_) | copy-start | bytes 786436
  78.0 4.7 %collective-permute-start.30 = (f32[512,128]{1,0:T(8,128)S(1)}, f32[512,128]{1,0:T(8,128)S(1)}, u32[]{:S(2)}, u32[]{:S(2)}) collective-permute-start(f32[512,128]{1,0:T(8,128)S(1)} %add.42.refs_5_), channel_id=1, source_target_pairs={{0,1},{1,0},{2,3},{3,2},{4,5},{5,4},{6,7},{7,6},{8,9},{9,8},{10,11... | collective-permute-start | bytes 786440 | tf_op jit(solution)/shard_map/ppermute | solution.py:390
  78.1 9.2 %collective-permute-start.26 = (f32[512,128]{1,0:T(8,128)S(1)}, f32[512,128]{1,0:T(8,128)S(1)}, u32[]{:S(2)}, u32[]{:S(2)}) collective-permute-start(f32[512,128]{1,0:T(8,128)S(1)} %add.42.refs_5_), channel_id=1, source_target_pairs={{0,2},{1,3},{2,0},{3,1},{4,6},{5,7},{6,4},{7,5},{8,10},{9,11},{10,... | collective-permute-start | bytes 786440 | tf_op jit(solution)/shard_map/ppermute | solution.py:390
  78.2 9.2 %collective-permute-start.19 = (f32[512,128]{1,0:T(8,128)S(1)}, f32[512,128]{1,0:T(8,128)S(1)}, u32[]{:S(2)}, u32[]{:S(2)}) collective-permute-start(f32[512,128]{1,0:T(8,128)S(1)} %add.42.refs_5_), channel_id=1, source_target_pairs={{0,4},{1,5},{2,6},{3,7},{4,0},{5,1},{6,2},{7,3},{8,12},{9,13},{10,... | collective-permute-start | bytes 786440 | tf_op jit(solution)/shard_map/ppermute | solution.py:390
  82.5 17.7 %copy-start.1 = (f32[512,128]{1,0:T(8,128)}, f32[512,128]{1,0:T(8,128)S(1)}, u32[]{:S(2)}) copy-start(f32[512,128]{1,0:T(8,128)S(1)} %add.41.refs_4_) | copy-start | bytes 786436
  82.5 10.4 %collective-permute-start.16 = (f32[512,128]{1,0:T(8,128)S(1)}, f32[512,128]{1,0:T(8,128)S(1)}, u32[]{:S(2)}, u32[]{:S(2)}) collective-permute-start(f32[512,128]{1,0:T(8,128)S(1)} %add.41.refs_4_), channel_id=1, source_target_pairs={{0,2},{1,3},{2,0},{3,1},{4,6},{5,7},{6,4},{7,5},{8,10},{9,11},{10,... | collective-permute-start | bytes 786440 | tf_op jit(solution)/shard_map/ppermute | solution.py:390
  82.6 10.4 %collective-permute-start.29 = (f32[512,128]{1,0:T(8,128)S(1)}, f32[512,128]{1,0:T(8,128)S(1)}, u32[]{:S(2)}, u32[]{:S(2)}) collective-permute-start(f32[512,128]{1,0:T(8,128)S(1)} %add.41.refs_4_), channel_id=1, source_target_pairs={{0,1},{1,0},{2,3},{3,2},{4,5},{5,4},{6,7},{7,6},{8,9},{9,8},{10,11... | collective-permute-start | bytes 786440 | tf_op jit(solution)/shard_map/ppermute | solution.py:390
  82.7 17.5 %copy-start.2 = (f32[512,128]{1,0:T(8,128)}, f32[512,128]{1,0:T(8,128)S(1)}, u32[]{:S(2)}) copy-start(f32[512,128]{1,0:T(8,128)S(1)} %collective-permute-done.30.refs_7_) | copy-start | bytes 786436
  82.7 10.4 %collective-permute-start.23 = (f32[512,128]{1,0:T(8,128)S(1)}, f32[512,128]{1,0:T(8,128)S(1)}, u32[]{:S(2)}, u32[]{:S(2)}) collective-permute-start(f32[512,128]{1,0:T(8,128)S(1)} %add.41.refs_4_), channel_id=1, source_target_pairs={{0,4},{1,5},{2,6},{3,7},{4,0},{5,1},{6,2},{7,3},{8,12},{9,13},{10,... | collective-permute-start | bytes 786440 | tf_op jit(solution)/shard_map/ppermute | solution.py:390
  87.4 15.3 %copy-start.5 = (f32[512,128]{1,0:T(8,128)}, f32[512,128]{1,0:T(8,128)S(1)}, u32[]{:S(2)}) copy-start(f32[512,128]{1,0:T(8,128)S(1)} %collective-permute-done.26.refs_5_) | copy-start | bytes 786436
  87.4 6.2 %collective-permute-start.28 = (f32[512,128]{1,0:T(8,128)S(1)}, f32[512,128]{1,0:T(8,128)S(1)}, u32[]{:S(2)}, u32[]{:S(2)}) collective-permute-start(f32[512,128]{1,0:T(8,128)S(1)} %collective-permute-done.26.refs_5_), channel_id=1, source_target_pairs={{0,1},{1,0},{2,3},{3,2},{4,5},{5,4},{6,7},{7,6},{8,9},{9,8},{10,11... | collective-permute-start | bytes 786440 | tf_op jit(solution)/shard_map/ppermute | solution.py:390
  87.4 17.6 %copy-start.4 = (f32[512,128]{1,0:T(8,128)}, f32[512,128]{1,0:T(8,128)S(1)}, u32[]{:S(2)}) copy-start(f32[512,128]{1,0:T(8,128)S(1)} %collective-permute-done.19.refs_5_) | copy-start | bytes 786436
  87.4 10.6 %collective-permute-start.20 = (f32[512,128]{1,0:T(8,128)S(1)}, f32[512,128]{1,0:T(8,128)S(1)}, u32[]{:S(2)}, u32[]{:S(2)}) collective-permute-start(f32[512,128]{1,0:T(8,128)S(1)} %collective-permute-done.19.refs_5_), channel_id=1, source_target_pairs={{0,2},{1,3},{2,0},{3,1},{4,6},{5,7},{6,4},{7,5},{8,10},{9,11},{10,... | collective-permute-start | bytes 786440 | tf_op jit(solution)/shard_map/ppermute | solution.py:390
  93.0 9.7 %copy-start.9 = (f32[512,128]{1,0:T(8,128)}, f32[512,128]{1,0:T(8,128)S(1)}, u32[]{:S(2)}) copy-start(f32[512,128]{1,0:T(8,128)S(1)} %collective-permute-done.16.refs_4_) | copy-start | bytes 786436
  93.0 7.2 %collective-permute-start.17 = (f32[512,128]{1,0:T(8,128)S(1)}, f32[512,128]{1,0:T(8,128)S(1)}, u32[]{:S(2)}, u32[]{:S(2)}) collective-permute-start(f32[512,128]{1,0:T(8,128)S(1)} %collective-permute-done.16.refs_4_), channel_id=1, source_target_pairs={{0,4},{1,5},{2,6},{3,7},{4,0},{5,1},{6,2},{7,3},{8,12},{9,13},{10,... | collective-permute-start | bytes 786440 | tf_op jit(solution)/shard_map/ppermute | solution.py:390
  93.0 9.7 %collective-permute-start.27 = (f32[512,128]{1,0:T(8,128)S(1)}, f32[512,128]{1,0:T(8,128)}, u32[]{:S(2)}, u32[]{:S(2)}) collective-permute-start(f32[512,128]{1,0:T(8,128)S(1)} %collective-permute-done.16.refs_4_), channel_id=1, source_target_pairs={{0,1},{1,0},{2,3},{3,2},{4,5},{5,4},{6,7},{7,6},{8,9},{9,8},{10,11... | collective-permute-start | bytes 786440 | tf_op jit(solution)/shard_map/ppermute | solution.py:390
  93.1 11.9 %copy-start.7 = (f32[512,128]{1,0:T(8,128)}, f32[512,128]{1,0:T(8,128)S(1)}, u32[]{:S(2)}) copy-start(f32[512,128]{1,0:T(8,128)S(1)} %collective-permute-done.23.refs_4_) | copy-start | bytes 786436
  93.1 11.9 %collective-permute-start.25 = (f32[512,128]{1,0:T(8,128)S(1)}, f32[512,128]{1,0:T(8,128)S(1)}, u32[]{:S(2)}, u32[]{:S(2)}) collective-permute-start(f32[512,128]{1,0:T(8,128)S(1)} %collective-permute-done.19.refs_5_), channel_id=1, source_target_pairs={{0,1},{1,0},{2,3},{3,2},{4,5},{5,4},{6,7},{7,6},{8,9},{9,8},{10,11... | collective-permute-start | bytes 786440 | tf_op jit(solution)/shard_map/ppermute | solution.py:390
  93.6 11.5 %collective-permute-start.24 = (f32[512,128]{1,0:T(8,128)S(1)}, f32[512,128]{1,0:T(8,128)}, u32[]{:S(2)}, u32[]{:S(2)}) collective-permute-start(f32[512,128]{1,0:T(8,128)S(1)} %collective-permute-done.23.refs_4_), channel_id=1, source_target_pairs={{0,1},{1,0},{2,3},{3,2},{4,5},{5,4},{6,7},{7,6},{8,9},{9,8},{10,11... | collective-permute-start | bytes 786440 | tf_op jit(solution)/shard_map/ppermute | solution.py:390
  98.1 10.0 %collective-permute-start.22 = (f32[512,128]{1,0:T(8,128)S(1)}, f32[512,128]{1,0:T(8,128)S(1)}, u32[]{:S(2)}, u32[]{:S(2)}) collective-permute-start(f32[512,128]{1,0:T(8,128)S(1)} %collective-permute-done.20.refs_5_), channel_id=1, source_target_pairs={{0,1},{1,0},{2,3},{3,2},{4,5},{5,4},{6,7},{7,6},{8,9},{9,8},{10,11... | collective-permute-start | bytes 786440 | tf_op jit(solution)/shard_map/ppermute | solution.py:390
  100.2 7.8 %collective-permute-start.21 = (f32[512,128]{1,0:T(8,128)S(1)}, f32[512,128]{1,0:T(8,128)}, u32[]{:S(2)}, u32[]{:S(2)}) collective-permute-start(f32[512,128]{1,0:T(8,128)S(1)} %collective-permute-done.17.refs_4_), channel_id=1, source_target_pairs={{0,1},{1,0},{2,3},{3,2},{4,5},{5,4},{6,7},{7,6},{8,9},{9,8},{10,11... | collective-permute-start | bytes 786440 | tf_op jit(solution)/shard_map/ppermute | solution.py:390
  (12 other events, 42.3 us)
where the time goes:
time: 111 us
  waiting for transfers between devices  49.4 us (45%)
  Pallas kernels  32.6 us (29%)
  starting transfers between devices  24.1 us (22%)
  other arithmetic  2.65 us (2%)
  local copies, waits for them, and re-layouts  2.01 us (2%)
    ppermute x31, waiting for transfers between devices, permute(): return lax.ppermute(x, 'tile', [(i, target(i)) for i in range(devices)])  49.4 us
    ppermute x31, starting transfers between devices, permute(): return lax.ppermute(x, 'tile', [(i, target(i)) for i in range(devices)])  24.1 us
    pallas_call x1, Pallas kernels, match_and_warp(): pl.pallas_call(functools.partial(match_kernel, strips=strips, parts=parts...  17.6 us
    pallas_call x4, Pallas kernels, finish(): pl.pallas_call(functools.partial(finish_kernel, visits=visits, parts=part...  9.34 us
    pallas_call x2, Pallas kernels, reduce_blocks(): pl.pallas_call(kernel, in_specs=[smem, smem] + [vmem] * (1 + len(pieces)...  5.59 us
  transfers between devices with their start and end apart: 31, of which 14 were waited for; matrix products, arithmetic and copies ran while one was open for 2% of the time, Pallas kernels for 9%

commit v1 on v0

v1 whole, which is shorter than its diff:
```python
import functools
import jax
import jax.numpy as jnp
from jax import lax
from jax.experimental import pallas as pl
from jax.experimental.pallas import tpu as pltpu
from jax.sharding import PartitionSpec as P


BLOCK = 128
LANES = 128
SEG = 32


def skew(rows8, base):
    base = base % LANES
    if base > LANES - 8:
        rows8 = pltpu.roll(rows8, 8, 1)
        base -= 8
    return pltpu.roll(rows8, base, 1, stride=1, stride_axis=0)


def iotas(rows):
    lane = lax.broadcasted_iota(jnp.int32, (rows, LANES), 1)
    row = lax.broadcasted_iota(jnp.int32, (rows, LANES), 0)
    return lane, lane - row


def split(x):
    high = x.astype(jnp.bfloat16)
    low = (x - high.astype(jnp.float32)).astype(jnp.bfloat16)
    return high, low


def banded_rows(tap_row, length, taps, first):
    _, diff = iotas(8)
    wide = jnp.broadcast_to(tap_row, (8, LANES))
    tiles = []
    for start in range(0, length, 8):
        rolled = skew(wide, start + first)
        cols = []
        for tile in range(length // LANES):
            k = diff + (LANES * tile - start - first)
            cols.append(jnp.where((k >= 0) & (k < taps), rolled, 0.0))
        tiles.append(jnp.concatenate(cols, axis=1) if len(cols) > 1 else cols[0])
    return jnp.concatenate(tiles, axis=0)


def as_column(row):
    count = row.shape[1]
    lane = lax.broadcasted_iota(jnp.int32, (count, count), 1)
    index = lax.broadcasted_iota(jnp.int32, (count, count), 0)
    return jnp.sum(jnp.where(lane == index, row, 0.0), axis=1, keepdims=True)


def sinc(x):
    angle = jnp.where(x == 0, 1.0, jnp.pi * x)
    return jnp.where(x == 0, 1.0, jnp.sin(angle) / angle)


def banded_region(tap_row, rows, width, taps, first, offset, span):
    lane, diff = iotas(8)
    wide = jnp.broadcast_to(tap_row, (8, LANES))
    chunks = []
    for start in range(0, rows, 8):
        lead = start + first + offset
        rolled = skew(wide, lead)
        cols = []
        for tile in range(width // LANES):
            begin = LANES * tile
            k = diff + (begin - lead)
            keep = (k >= 0) & (k < taps) & (lane >= offset - begin) & (lane < offset + span - begin)
            cols.append(jnp.where(keep, rolled, 0.0))
        chunks.append(jnp.concatenate(cols, axis=1))
    return jnp.concatenate(chunks, axis=0)


def fill_matched_coefficients(step, table, h_win, side, filters, taps, length, win):
    half = length // 2
    middle = taps // 2
    origin = side * (length - win)
    lane, diff = iotas(8)
    tiles = -(-filters * SEG // LANES)
    terms = [
        [jnp.broadcast_to(table[6 * t + j, pl.ds(step, 1), :], (8, LANES)) for j in range(6)]
        for t in range(tiles)
    ]
    for group in range(half // 16):
        halves = []
        for sub in range(2):
            start = 16 * group + 8 * sub
            row = lax.broadcasted_iota(jnp.int32, (8, LANES), 0) + (side * half + start)
            u = 2.0 * row.astype(jnp.float32) / (length - 1) - 1.0
            compact = {}
            for tile in range(tiles):
                t = terms[tile]
                compact[0, tile] = t[0] + u * (t[1] + u * t[3])
                compact[1, tile] = t[2] + u * t[4]
                compact[2, tile] = t[5]
            acc = {}
            for b in range(filters):
                lead = b * win + side * half + start - middle - origin
                first = max(lead, b * win)
                last = min(lead + 7 + taps - 1, (b + 1) * win - 1)
                masks = {}
                for tile in range(first // LANES, last // LANES + 1):
                    k = diff + (LANES * tile - lead)
                    mask = (k >= 0) & (k < taps)
                    if lead < b * win:
                        mask &= lane >= b * win - LANES * tile
                    if lead + 7 + taps > (b + 1) * win:
                        mask &= lane < (b + 1) * win - LANES * tile
                    masks[tile] = mask
                source, off = divmod(b * SEG, LANES)
                for q in range(3):
                    rolled = skew(compact[q, source], lead - off)
                    for tile, mask in masks.items():
                        acc[q, tile] = jnp.where(mask, rolled, acc.get((q, tile), 0.0))
            halves.append(acc)
        for q, tile in sorted(set(halves[0]) | set(halves[1])):
            zero = jnp.zeros((8, LANES), jnp.float32)
            both = jnp.concatenate([h.get((q, tile), zero) for h in halves], axis=0)
            h_win[
                side,
                q * half + 16 * group : q * half + 16 * group + 16,
                tile * LANES : (tile + 1) * LANES,
            ] = both.astype(jnp.bfloat16)


def match_kernel(x_ref, c_ref, rtap_ref, ctap_ref, out_ref, pow_ref, *refs, pack, visits):
    rbig, tap_rows, basis, table = refs[:4]
    s_wins = refs[4 : 4 + pack]
    h_wins = refs[4 + pack :]
    filters, taps = rtap_ref.shape
    length = x_ref.shape[1]
    half = length // 2
    middle = taps // 2
    win = -(-(half + middle) // 16) * 16
    step = pl.program_id(0)

    @pl.when(step == 0)
    def _():
        tap_rows[...] = jnp.zeros(tap_rows.shape, jnp.float32)
        tap_rows[0:filters, 0:taps] = rtap_ref[...].astype(jnp.float32)
        tap_rows[8 : 8 + filters, 0:taps] = ctap_ref[...].astype(jnp.float32)
        i = lax.broadcasted_iota(jnp.int32, (LANES, LANES), 0)
        j = lax.broadcasted_iota(jnp.int32, (LANES, LANES), 1)
        flip = (i + j == taps - 1).astype(jnp.float32).astype(jnp.bfloat16)
        flipped = jnp.dot(
            tap_rows[0:8, :].astype(jnp.bfloat16), flip, preferred_element_type=jnp.float32
        )
        for b in range(filters):
            band = banded_rows(flipped[b : b + 1, :], length, taps, -middle)
            rbig[:, b * length : (b + 1) * length] = band.astype(jnp.bfloat16)
        for ref in (*s_wins, *h_wins):
            ref[...] = jnp.zeros(ref.shape, jnp.bfloat16)
        pow_ref[...] = jnp.zeros(pow_ref.shape, jnp.float32)
        basis[...] = jnp.zeros(basis.shape, jnp.float32)
        for a in range(filters):
            row = jnp.broadcast_to(tap_rows[8 + a : 9 + a, :], (8, LANES))
            for b in range(filters):
                tile, off = divmod(b * SEG, LANES)
                moved = pltpu.roll(row, off, 1) if off else row
                basis[a * filters + b : a * filters + b + 1, tile * LANES : (tile + 1) * LANES] = (
                    moved[0:1]
                )
        count, terms = c_ref.shape[1:]
        for tile in range(basis.shape[1] // LANES):
            table[6 * tile : 6 * tile + 6] = jnp.dot(
                c_ref[...].reshape(6 * count, terms),
                basis[0:terms, tile * LANES : (tile + 1) * LANES],
                precision=lax.Precision.HIGHEST,
                preferred_element_type=jnp.float32,
            ).reshape(6, count, LANES)

    col = lax.broadcasted_iota(jnp.int32, (1, length), 1).astype(jnp.float32)
    w = 2.0 * col / (length - 1) - 1.0

    def smooth(n):
        image = x_ref[n].astype(jnp.bfloat16)
        for b in range(filters):
            part = jnp.dot(
                image, rbig[:, b * length : (b + 1) * length], preferred_element_type=jnp.float32
            ).astype(jnp.bfloat16)
            s_wins[n][0, b * win : (b + 1) * win, :] = part[0:win]
            s_wins[n][1, b * win : (b + 1) * win, :] = part[length - win :]

    def fill(n, side):
        fill_matched_coefficients(
            step * pack + n, table, h_wins[n], side, filters, taps, length, win
        )

    def combine(n, side):
        z = jnp.dot(h_wins[n][side], s_wins[n][side], preferred_element_type=jnp.float32)
        matched = z[0:half] + w * (z[half : 2 * half] + w * z[2 * half :])
        out_ref[n, side * half : (side + 1) * half, :] = matched
        squares = jnp.sum(matched * matched, axis=0, keepdims=True)
        visit = pl.ds((step * pack + n) % visits, 1)
        pow_ref[visit, :] = pow_ref[visit, :] + (squares[:, :half] + squares[:, half:])

    smooth(0)
    fill(0, 0)
    for n in range(pack):
        if n + 1 < pack:
            smooth(n + 1)
        fill(n, 1)
        combine(n, 0)
        if n + 1 < pack:
            fill(n + 1, 0)
        combine(n, 1)


def match(images, coeffs, row_taps, col_taps, visits):
    count, length, _ = images.shape
    filters, taps = row_taps.shape
    half = length // 2
    win = -(-(half + taps // 2) // 16) * 16
    depth = -(-filters * win // LANES) * LANES
    pow_rows = -(-visits // 8) * 8
    pack = 2 - count % 2
    tiles = -(-filters * SEG // LANES)
    return pl.pallas_call(
        functools.partial(match_kernel, pack=pack, visits=visits),
        grid=(count // pack,),
        in_specs=[
            pl.BlockSpec((pack, length, length), lambda i: (i, 0, 0)),
            pl.BlockSpec(coeffs.shape, lambda i: (0, 0, 0)),
            pl.BlockSpec(row_taps.shape, lambda i: (0, 0)),
            pl.BlockSpec(col_taps.shape, lambda i: (0, 0)),
        ],
        out_specs=[
            pl.BlockSpec((pack, length, length), lambda i: (i, 0, 0)),
            pl.BlockSpec((pow_rows, LANES), lambda i: (0, 0)),
        ],
        out_shape=[
            jax.ShapeDtypeStruct((count, length, length), jnp.float32),
            jax.ShapeDtypeStruct((pow_rows, LANES), jnp.float32),
        ],
        scratch_shapes=[
            pltpu.VMEM((length, filters * length), jnp.bfloat16),
            pltpu.VMEM((16, LANES), jnp.float32),
            pltpu.VMEM((-(-filters * filters // 8) * 8, tiles * LANES), jnp.float32),
            pltpu.VMEM((6 * tiles, count, LANES), jnp.float32),
        ]
        + [pltpu.VMEM((2, depth, length), jnp.bfloat16)] * pack
        + [pltpu.VMEM((2, 3 * half, depth), jnp.bfloat16)] * pack,
        name="match",
    )(images, coeffs, row_taps, col_taps)


def warp_kernel(own_ref, sub_ref, m_ref, *refs, strips, part, parts, pack, powers):
    given = refs[:powers]
    outs = refs[powers : powers + strips]
    shifts, held = refs[powers + strips :]
    step = pl.program_id(0)
    half = m_ref.shape[1] // 2
    rows = half // parts
    height = rows // strips
    low = max(part * rows - 3, 0) // 16 * 16
    span = min(-(-(part * rows + rows + 2) // 16) * 16, half) - low
    depth = -(-3 * span // LANES) * LANES

    @pl.when(step == 0)
    def _():
        lanes = lax.broadcasted_iota(jnp.int32, (1, LANES), 1).astype(jnp.float32)
        for axis, steps in enumerate((2.0 - lanes, lanes - 3.0)):
            distance = steps + as_column(sub_ref[axis : axis + 1, :])
            value = sinc(distance) * sinc(distance / 3.0)
            shifts[axis] = jnp.where(jnp.abs(distance) < 3.0, value, 0.0)

    lane = lax.broadcasted_iota(jnp.int32, (1, depth), 1)
    for n in range(pack):
        image = step * pack + n
        left = jnp.zeros((rows, depth), jnp.float32)
        for copy in range(3):
            left += banded_region(
                shifts[0, pl.ds(image, 1), :], rows, depth, 6, part * rows - low - 2, copy * span, span
            )
        high = left.astype(jnp.bfloat16).astype(jnp.float32)
        left = jnp.where(lane < 2 * span, high, left - high).astype(jnp.bfloat16)
        horizontal = split(banded_rows(shifts[1, pl.ds(image, 1), :], half, 6, -3))
        right = jnp.concatenate([horizontal[0], horizontal[0], horizontal[1]], axis=0)
        moved = []
        for side in range(2):
            upper, lower = split(m_ref[n, side * half + low : side * half + low + span, :])
            stacked = [upper, lower, upper]
            if depth > 3 * span:
                stacked.append(jnp.zeros((depth - 3 * span, 2 * half), jnp.bfloat16))
            full = jnp.dot(
                left, jnp.concatenate(stacked, axis=0), preferred_element_type=jnp.float32
            )
            moved += [full[:, :half], full[:, half:]]
        upper, lower = split(jnp.concatenate(moved, axis=0))
        lhs = jnp.concatenate([upper, lower, upper], axis=1)
        held[n] = jnp.dot(lhs, right, preferred_element_type=jnp.float32).reshape(4, rows, half)
    for n in range(pack):
        for k in range(strips):
            begin = pl.ds(pl.multiple_of((own_ref[0] ^ k) * height, height), height)
            for block in range(4):
                item = 4 * (step * pack + n) + block
                at = pl.ds(pl.multiple_of(item * height, height), height)
                outs[k][at, :] = held[n, block, begin, :]

    if powers:

        @pl.when(step == pl.num_programs(0) - 1)
        def _():
            total = given[0][...]
            for other in given[1:]:
                total = total + other[...]
            for out in outs:
                out[out.shape[0] - total.shape[0] :, :] = total


def warp(own, subpixel, matched, powers, part, parts, strips):
    count, length, _ = matched.shape
    half = length // 2
    rows = count * 4 * half // strips // parts + sum(p.shape[0] for p in powers[:1])
    pack = 2 - count % 2
    return pl.pallas_call(
        functools.partial(
            warp_kernel, strips=strips, part=part, parts=parts, pack=pack, powers=len(powers)
        ),
        grid_spec=pltpu.PrefetchScalarGridSpec(
            num_scalar_prefetch=1,
            grid=(count // pack,),
            in_specs=[
                pl.BlockSpec(subpixel.shape, lambda i, own: (0, 0)),
                pl.BlockSpec((pack, length, length), lambda i, own: (i, 0, 0)),
            ]
            + [pl.BlockSpec(p.shape, lambda i, own: (0, 0)) for p in powers],
            out_specs=[pl.BlockSpec((rows, half), lambda i, own: (0, 0))] * strips,
            scratch_shapes=[
                pltpu.VMEM((2, count, LANES), jnp.float32),
                pltpu.VMEM((pack, 4, half // parts, half), jnp.float32),
            ],
        ),
        out_shape=[jax.ShapeDtypeStruct((rows, half), jnp.float32)] * strips,
        name="warp",
    )(own, subpixel, matched, *powers)


def reduce_kernel(own_ref, dest_ref, slot_ref, *refs, strips, slots, images, visits, pixels):
    pieces = refs[:strips]
    given = refs[strips:-4]
    out_ref, var_ref, acc0, acc1 = refs[-4:]
    pow_rows = var_ref.shape[0]
    height = out_ref.shape[0] // slots
    if given:
        variance = given[0][...]
    else:
        total = pieces[0][pieces[0].shape[0] - pow_rows :, :]
        for piece in pieces[1:]:
            total = total + piece[piece.shape[0] - pow_rows :, :]
        total = jnp.sum(total, axis=1, keepdims=True)
        variance = jnp.broadcast_to(total / pixels + 1e-05, (pow_rows, LANES))
    var_ref[...] = variance
    weight = 1.0 / variance
    acc0[...] = jnp.zeros(acc0.shape, jnp.float32)
    acc1[...] = jnp.zeros(acc1.shape, jnp.float32)
    own = own_ref[0]
    for image in range(images):
        visit = image % visits
        scale = jnp.broadcast_to(weight[visit : visit + 1], (height, LANES))
        for k in range(strips):
            for block in range(4):
                item = 4 * image + block
                acc = acc0 if block % 2 == 0 else acc1
                slot = dest_ref[own ^ k, item]
                at = pl.ds(pl.multiple_of(slot * height, height), height)
                rows = slice(item * height, (item + 1) * height)
                acc[at, :] = acc[at, :] + scale * pieces[k][rows, :]
    devices, items = slot_ref.shape
    lane = lax.broadcasted_iota(jnp.int32, (pow_rows, items), 1)
    row = lax.broadcasted_iota(jnp.int32, (pow_rows, items), 0)
    by_item = jnp.sum(
        jnp.where(lane // 4 % visits == row, weight[:, 0:1], 0.0), axis=0, keepdims=True
    )
    index = lax.broadcasted_iota(jnp.int32, (slots, items), 0)
    hits = jnp.zeros((slots, items), jnp.float32)
    for device in range(devices):
        hits = hits + jnp.where(slot_ref[device : device + 1, :] == index, 1.0, 0.0)
    denom = jnp.sum(hits * by_item, axis=1, keepdims=True)
    inverse = 1.0 / jnp.where(denom > 0, denom, 1.0)
    for slot in range(slots):
        at = slice(slot * height, (slot + 1) * height)
        scale = jnp.broadcast_to(inverse[slot : slot + 1, :], (height, LANES))
        out_ref[at, :] = (acc0[at, :] + acc1[at, :]) * scale


def reduce_blocks(own, dest, pieces, variance, slots, images, visits, pixels):
    pow_rows = -(-visits // 8) * 8
    given = [] if variance is None else [variance]
    height = pieces[0].shape[0] // (images * 4)
    smem = pl.BlockSpec(memory_space=pltpu.SMEM)
    vmem = pl.BlockSpec(memory_space=pltpu.VMEM)
    kernel = functools.partial(
        reduce_kernel,
        strips=len(pieces),
        slots=slots,
        images=images,
        visits=visits,
        pixels=pixels,
    )
    return pl.pallas_call(
        kernel,
        in_specs=[smem, smem] + [vmem] * (1 + len(pieces) + len(given)),
        out_specs=[vmem, vmem],
        out_shape=[
            jax.ShapeDtypeStruct((slots * height, LANES), jnp.float32),
            jax.ShapeDtypeStruct((pow_rows, LANES), jnp.float32),
        ],
        scratch_shapes=[pltpu.VMEM((slots * height, LANES), jnp.float32)] * 2,
        name="reduce_blocks",
    )(own, dest, dest, *pieces, *given)


def finish_kernel(own_ref, dest_ref, var_ref, *refs, strips, visits):
    warped = refs[:strips]
    templates = refs[strips : 2 * strips]
    out_ref = refs[-1]
    own = own_ref[0]
    height = out_ref.shape[2] // strips
    inverse = 1.0 / jnp.sqrt(var_ref[...])
    for image in range(out_ref.shape[0]):
        visit = image % visits
        scale = jnp.broadcast_to(inverse[visit : visit + 1, :], (height, LANES))
        for block in range(4):
            item = 4 * image + block
            at = pl.ds(pl.multiple_of(dest_ref[own, item] * height, height), height)
            for k in range(strips):
                here = warped[k][item * height : (item + 1) * height, :]
                rows = pl.ds(pl.multiple_of(((own % strips) ^ k) * height, height), height)
                out_ref[image, block, rows, :] = (here - templates[k][at, :]) * scale


def finish(own, dest, variance, warped, templates, previous, part, images, visits):
    strips = len(warped)
    smem = pl.BlockSpec(memory_space=pltpu.SMEM)
    vmem = pl.BlockSpec(memory_space=pltpu.VMEM)
    extra = [] if previous is None else [previous]
    inputs = [variance, *warped, *templates]
    return pl.pallas_call(
        functools.partial(finish_kernel, strips=strips, visits=visits),
        grid=(1,),
        in_specs=[smem, smem]
        + [vmem] * len(inputs)
        + [pl.BlockSpec(memory_space=pl.ANY) for _ in extra],
        out_specs=pl.BlockSpec((images, 4, BLOCK // PARTS, LANES), lambda i: (0, 0, part, 0)),
        out_shape=jax.ShapeDtypeStruct((images, 4, BLOCK, LANES), jnp.float32),
        input_output_aliases={2 + len(inputs): 0} if extra else {},
        name="finish",
    )(own, dest, *inputs, *extra)


GROUP = 8
PARTS = 2


def per_device(exposures, row_taps, col_taps, kernel_coeffs, subpixel, destination):
    tile_count, visits, length = exposures.shape[:3]
    filters, _ = row_taps.shape
    devices = lax.axis_size("tile")
    own = lax.axis_index("tile").astype(jnp.int32).reshape(1)
    images = tile_count * visits
    slots = tile_count * devices * 4
    pixels = tile_count * devices * length * length
    dest = destination.reshape(devices, images * 4)

    def permute(x, target):
        return lax.ppermute(x, "tile", [(i, target(i)) for i in range(devices)])

    def swap(x, k):
        return permute(x, lambda i: i ^ k)

    def ahead(x, groups):
        return permute(x, lambda i: (i + groups * GROUP) % devices)

    others = devices // GROUP
    matched, power = match(
        exposures.reshape(images, length, length),
        kernel_coeffs.transpose(3, 0, 1, 2).reshape(-1, images, filters * filters),
        row_taps,
        col_taps,
        visits,
    )
    powers = [power] + [ahead(power, r) for r in range(1, others)]
    shifts = subpixel.transpose(2, 0, 1).reshape(2, images)
    warped = []
    pieces = []
    for part in range(PARTS):
        mine = warp(
            own % GROUP, shifts, matched, [] if part else powers, part, PARTS, GROUP
        )
        warped.append(mine)
        pieces.append([mine[0]] + [swap(mine[k], k) for k in range(1, GROUP)])
    full = []
    variance = None
    for part in range(PARTS):
        partial, variance = reduce_blocks(
            own, dest, pieces[part], variance, slots, images, visits, pixels
        )
        moved = [ahead(partial, r) for r in range(1, others)]
        template = partial
        for piece in moved:
            template = template + piece
        two = swap(template, 2)
        four = swap(template, 4)
        six = swap(template, 6)
        full.append(
            [template, swap(template, 1)]
            + [two, swap(two, 1)]
            + [four, swap(four, 1)]
            + [six, swap(six, 1)]
        )
    result = None
    for part in range(PARTS):
        result = finish(own, dest, variance, warped[part], full[part], result, part, images, visits)
    return result.reshape(tile_count, visits, 4, BLOCK, BLOCK)


def solution(mesh):
    return jax.shard_map(
        per_device,
        mesh=mesh,
        in_specs=(
            P(("groups", "tile"), None, None, None),
            P(),
            P(),
            P(("groups", "tile"), None, None, None),
            P(("groups", "tile"), None, None),
            P("groups", None),
        ),
        out_specs=P(("groups", "tile"), None, None, None, None),
        check_vma=False,
    )
```

time: 111 us -> 108 us (0.973)
  waiting for transfers between devices: 49.4 us -> 42.3 us
  starting transfers between devices: 24.1 us -> 29.2 us
  Pallas kernels: 32.6 us -> 30.2 us
  local copies, waits for them, and re-layouts: 2.01 us -> 4.04 us
    ppermute x31, waiting for transfers between devices: 49.4 us -> 42.3 us  [permute(): return lax.ppermute(x, 'tile', [(i, target(i)) for i in range(devices)])]
    ppermute x31, starting transfers between devices: 24.1 us -> 29.2 us  [permute(): return lax.ppermute(x, 'tile', [(i, target(i)) for i in range(devices)])]
    pallas_call x5, Pallas kernels: 27 us -> 24.7 us  [the longest x2 10.7 us: warp(): pl.pallas_call(functools.partial(warp_kernel, strips=strips, part=part, p...]
    unnamed x58 -> x60, local copies, waits for them, and re-layouts: 2.01 us -> 4.04 us
  transfers between devices with their start and end apart: 31 -> 31, of which waited for: 14 -> 14; matrix products, arithmetic and copies ran while one was open for 2% -> 2% of each run, Pallas kernels for 9% -> 13%
where the time goes in v1:
time: 108 us
  waiting for transfers between devices  42.3 us (39%)
  Pallas kernels  30.2 us (28%)
  starting transfers between devices  29.2 us (27%)
  local copies, waits for them, and re-layouts  4.04 us (4%)
  other arithmetic  1.96 us (2%)
    ppermute x31, waiting for transfers between devices, permute(): return lax.ppermute(x, 'tile', [(i, target(i)) for i in range(devices)])  42.3 us
    ppermute x31, starting transfers between devices, permute(): return lax.ppermute(x, 'tile', [(i, target(i)) for i in range(devices)])  29.2 us
    pallas_call x2, Pallas kernels, warp(): pl.pallas_call(functools.partial(warp_kernel, strips=strips, part=part, p...  10.7 us
    pallas_call x1, Pallas kernels, match(): pl.pallas_call(functools.partial(match_kernel, pack=pack, visits=visits),...  7.8 us
    pallas_call x2, Pallas kernels, finish(): pl.pallas_call(functools.partial(finish_kernel, strips=strips, visits=vis...  6.23 us
    pallas_call x2, Pallas kernels, reduce_blocks(): pl.pallas_call(kernel, in_specs=[smem, smem] + [vmem] * (1 + len(pieces)...  5.55 us
    unnamed x60, local copies, waits for them, and re-layouts  4.04 us
  transfers between devices with their start and end apart: 31, of which 14 were waited for; matrix products, arithmetic and copies ran while one was open for 2% of the time, Pallas kernels for 13%

profile of v1, /device:TPU:0, one launch (start us, length us, event | category | flops | bytes accessed | tf_op | source)
XLA Modules:
  0.0 108.1 jit_solution(5890875602813404893)
XLA Ops:
  0.0 7.8 %match.1 = (f32[8,256,256]{2,1,0:T(8,128)}, f32[8,128]{1,0:T(8,128)}) custom-call(f32[8,256,256]{2,1,0:T(8,128)} %bitcast.9, f32[6,8,25]{2,1,0:T(8,128)} %bitcast.10, bf16[5,21]{1,0:T(8,128)(2,1)} %rtap_ref.1, bf16[5,21]{1,0:T(8,128)(2,1)} %ctap_ref.1), custom_call_target="tpu_custom_call" | custom-call | tf_op jit(solution)/shard_map/match/pallas_call | solution.py:222
  7.8 4.1 %collective-permute-start.7 = (f32[8,128]{1,0:T(8,128)}, f32[8,128]{1,0:T(8,128)S(1)}, u32[]{:S(2)}, u32[]{:S(2)}) collective-permute-start(f32[8,128]{1,0:T(8,128)} %get-tuple-element.36.refs_0_), channel_id=1, source_target_pairs={{0,8},{1,9},{2,10},{3,11},{4,12},{5,13},{6,14},{7,15},{8,0},{9,1},... | collective-permute-start | bytes 12296 | tf_op jit(solution)/shard_map/ppermute | solution.py:471
  11.9 1.8 %collective-permute-done.7.refs_1_ = f32[8,128]{1,0:T(8,128)S(1)} collective-permute-done((f32[8,128]{1,0:T(8,128)}, f32[8,128]{1,0:T(8,128)S(1)}, u32[]{:S(2)}, u32[]{:S(2)}) %collective-permute-start.7) | collective-permute-done | bytes 4128 | tf_op jit(solution)/shard_map/ppermute | solution.py:471
  13.7 0.6 copy-done.29
  14.2 5.4 %warp.3 = (f32[264,128]{1,0:T(8,128)}, f32[264,128]{1,0:T(8,128)}, f32[264,128]{1,0:T(8,128)}, f32[264,128]{1,0:T(8,128)}, f32[264,128]{1,0:T(8,128)}, /*index=5...) custom-call(s32[1]{0:T(128)S(6)} %select_n.9.own_ref, f32[2,8]{1,0:T(2,128)} %bitcast.11, ...), custom_call_target="tpu_custom_call" | custom-call | tf_op jit(solution)/shard_map/warp/pallas_call | solution.py:320
  19.8 1.8 %collective-permute-start.11 = (f32[264,128]{1,0:T(8,128)}, f32[264,128]{1,0:T(8,128)S(1)}, u32[]{:S(2)}, u32[]{:S(2)}) collective-permute-start(f32[264,128]{1,0:T(8,128)} %get-tuple-element.41.refs_4_), channel_id=1, source_target_pairs={{0,4},{1,5},{2,6},{3,7},{4,0},{5,1},{6,2},{7,3},{8,12},{9,13},{10,... | collective-permute-start | bytes 405512 | tf_op jit(solution)/shard_map/ppermute | solution.py:471
  21.6 1.4 %collective-permute-start.12 = (f32[264,128]{1,0:T(8,128)}, f32[264,128]{1,0:T(8,128)S(1)}, u32[]{:S(2)}, u32[]{:S(2)}) collective-permute-start(f32[264,128]{1,0:T(8,128)} %get-tuple-element.42.refs_5_), channel_id=1, source_target_pairs={{0,5},{1,4},{2,7},{3,6},{4,1},{5,0},{6,3},{7,2},{8,13},{9,12},{10,... | collective-permute-start | bytes 405512 | tf_op jit(solution)/shard_map/ppermute | solution.py:471
  22.9 1.5 %collective-permute-start.13 = (f32[264,128]{1,0:T(8,128)}, f32[264,128]{1,0:T(8,128)S(1)}, u32[]{:S(2)}, u32[]{:S(2)}) collective-permute-start(f32[264,128]{1,0:T(8,128)} %get-tuple-element.43.refs_6_), channel_id=1, source_target_pairs={{0,6},{1,7},{2,4},{3,5},{4,2},{5,3},{6,0},{7,1},{8,14},{9,15},{10,... | collective-permute-start | bytes 405512 | tf_op jit(solution)/shard_map/ppermute | solution.py:471
  24.5 0.7 collective-permute-start.14
  25.3 0.7 collective-permute-start.8
  26.0 2.2 %collective-permute-start.9 = (f32[264,128]{1,0:T(8,128)}, f32[264,128]{1,0:T(8,128)S(1)}, u32[]{:S(2)}, u32[]{:S(2)}) collective-permute-start(f32[264,128]{1,0:T(8,128)} %get-tuple-element.39.refs_2_), channel_id=1, source_target_pairs={{0,2},{1,3},{2,0},{3,1},{4,6},{5,7},{6,4},{7,5},{8,10},{9,11},{10,... | collective-permute-start | bytes 405512 | tf_op jit(solution)/shard_map/ppermute | solution.py:471
  28.2 5.3 %warp.2 = (f32[256,128]{1,0:T(8,128)}, f32[256,128]{1,0:T(8,128)}, f32[256,128]{1,0:T(8,128)}, f32[256,128]{1,0:T(8,128)}, f32[256,128]{1,0:T(8,128)}, /*index=5...) custom-call(s32[1]{0:T(128)S(6)} %select_n.9.own_ref, f32[2,8]{1,0:T(2,128)} %bitcast.12, ...), custom_call_target="tpu_custom_call" | custom-call | tf_op jit(solution)/shard_map/warp/pallas_call | solution.py:320
  33.7 1.6 %collective-permute-done.14.refs_7_ = f32[264,128]{1,0:T(8,128)S(1)} collective-permute-done((f32[264,128]{1,0:T(8,128)}, f32[264,128]{1,0:T(8,128)S(1)}, u32[]{:S(2)}, u32[]{:S(2)}) %collective-permute-start.14) | collective-permute-done | bytes 135200 | tf_op jit(solution)/shard_map/ppermute | solution.py:471
  35.3 0.9 collective-permute-start.2
  36.2 2.2 %collective-permute-done.9.refs_2_ = f32[264,128]{1,0:T(8,128)S(1)} collective-permute-done((f32[264,128]{1,0:T(8,128)}, f32[264,128]{1,0:T(8,128)S(1)}, u32[]{:S(2)}, u32[]{:S(2)}) %collective-permute-start.9) | collective-permute-done | bytes 135200 | tf_op jit(solution)/shard_map/ppermute | solution.py:471
  38.4 0.6 copy-done.21
  39.0 2.8 %reduce_blocks.2 = (f32[512,128]{1,0:T(8,128)}, f32[8,128]{1,0:T(8,128)}) custom-call(s32[1]{0:T(128)} %bitcast.own_ref, s32[16,32]{1,0:T(8,128)} %dest_ref.7, s32[16,32]{1,0:T(8,128)} %dest_ref.7, f32[264,128]{1,0:T(8,128)} %get-tuple-element.37.refs_0_, f32[264,128]{1,0:T(8,128)} %copy-done.20, f32[264,128]{1,0:T(8,128)} %copy-done.21, ...), custom_call_target="tpu_custom_call" | custom-call | tf_op jit(solution)/shard_map/reduce_blocks/pallas_call | solution.py:405
  41.8 2.8 %collective-permute-start.23 = (f32[512,128]{1,0:T(8,128)}, f32[512,128]{1,0:T(8,128)S(1)}, u32[]{:S(2)}, u32[]{:S(2)}) collective-permute-start(f32[512,128]{1,0:T(8,128)} %get-tuple-element.48), channel_id=1, source_target_pairs={{0,8},{1,9},{2,10},{3,11},{4,12},{5,13},{6,14},{7,15},{8,0},{9,1},... | collective-permute-start | bytes 786440 | tf_op jit(solution)/shard_map/ppermute | solution.py:471
  44.6 1.6 %collective-permute-start.3 = (f32[256,128]{1,0:T(8,128)}, f32[256,128]{1,0:T(8,128)S(1)}, u32[]{:S(2)}, u32[]{:S(2)}) collective-permute-start(f32[256,128]{1,0:T(8,128)} %get-tuple-element.32.refs_4_), channel_id=1, source_target_pairs={{0,4},{1,5},{2,6},{3,7},{4,0},{5,1},{6,2},{7,3},{8,12},{9,13},{10,... | collective-permute-start | bytes 393224 | tf_op jit(solution)/shard_map/ppermute | solution.py:471
  46.2 1.3 %collective-permute-start.5 = (f32[256,128]{1,0:T(8,128)}, f32[256,128]{1,0:T(8,128)S(1)}, u32[]{:S(2)}, u32[]{:S(2)}) collective-permute-start(f32[256,128]{1,0:T(8,128)} %get-tuple-element.34.refs_6_), channel_id=1, source_target_pairs={{0,6},{1,7},{2,4},{3,5},{4,2},{5,3},{6,0},{7,1},{8,14},{9,15},{10,... | collective-permute-start | bytes 393224 | tf_op jit(solution)/shard_map/ppermute | solution.py:471
  47.4 1.6 %collective-permute-start.6 = (f32[256,128]{1,0:T(8,128)}, f32[256,128]{1,0:T(8,128)S(1)}, u32[]{:S(2)}, u32[]{:S(2)}) collective-permute-start(f32[256,128]{1,0:T(8,128)} %get-tuple-element.35.refs_7_), channel_id=1, source_target_pairs={{0,7},{1,6},{2,5},{3,4},{4,3},{5,2},{6,1},{7,0},{8,15},{9,14},{10,... | collective-permute-start | bytes 393224 | tf_op jit(solution)/shard_map/ppermute | solution.py:471
  49.0 5.5 %collective-permute-done.3.refs_4_ = f32[256,128]{1,0:T(8,128)S(1)} collective-permute-done((f32[256,128]{1,0:T(8,128)}, f32[256,128]{1,0:T(8,128)S(1)}, u32[]{:S(2)}, u32[]{:S(2)}) %collective-permute-start.3) | collective-permute-done | bytes 131104 | tf_op jit(solution)/shard_map/ppermute | solution.py:471
  54.4 2.8 %collective-permute-done.4.refs_5_ = f32[256,128]{1,0:T(8,128)S(1)} collective-permute-done((f32[256,128]{1,0:T(8,128)}, f32[256,128]{1,0:T(8,128)S(1)}, u32[]{:S(2)}, u32[]{:S(2)}) %collective-permute-start.4) | collective-permute-done | bytes 131104 | tf_op jit(solution)/shard_map/ppermute | solution.py:471
  57.2 4.2 %collective-permute-done.5.refs_6_ = f32[256,128]{1,0:T(8,128)S(1)} collective-permute-done((f32[256,128]{1,0:T(8,128)}, f32[256,128]{1,0:T(8,128)S(1)}, u32[]{:S(2)}, u32[]{:S(2)}) %collective-permute-start.5) | collective-permute-done | bytes 131104 | tf_op jit(solution)/shard_map/ppermute | solution.py:471
  61.4 1.1 %collective-permute-done.6.refs_7_ = f32[256,128]{1,0:T(8,128)S(1)} collective-permute-done((f32[256,128]{1,0:T(8,128)}, f32[256,128]{1,0:T(8,128)S(1)}, u32[]{:S(2)}, u32[]{:S(2)}) %collective-permute-start.6) | collective-permute-done | bytes 131104 | tf_op jit(solution)/shard_map/ppermute | solution.py:471
  62.6 0.6 copy-done.28
  63.2 2.8 %reduce_blocks.3 = (f32[512,128]{1,0:T(8,128)}, f32[8,128]{1,0:T(8,128)}) custom-call(s32[1]{0:T(128)} %bitcast.own_ref, s32[16,32]{1,0:T(8,128)} %dest_ref.7, s32[16,32]{1,0:T(8,128)} %dest_ref.7, f32[256,128]{1,0:T(8,128)} %get-tuple-element.28.refs_0_, f32[256,128]{1,0:T(8,128)} %copy-done.22, f32[256,128]{1,0:T(8,128)} %copy-done.23, ...), custom_call_target="tpu_custom_call" | custom-call | tf_op jit(solution)/shard_map/reduce_blocks/pallas_call | solution.py:405
  66.0 1.0 collective-permute-start.15
  67.0 1.0 add.16.refs_8_
  68.0 1.3 %collective-permute-start.25 = (f32[512,128]{1,0:T(8,128)S(1)}, f32[512,128]{1,0:T(8,128)S(1)}, u32[]{:S(2)}, u32[]{:S(2)}) collective-permute-start(f32[512,128]{1,0:T(8,128)S(1)} %add.16.refs_8_), channel_id=1, source_target_pairs={{0,2},{1,3},{2,0},{3,1},{4,6},{5,7},{6,4},{7,5},{8,10},{9,11},{10,... | collective-permute-start | bytes 786440 | tf_op jit(solution)/shard_map/ppermute | solution.py:471
  69.3 1.5 %collective-permute-start.27 = (f32[512,128]{1,0:T(8,128)S(1)}, f32[512,128]{1,0:T(8,128)S(1)}, u32[]{:S(2)}, u32[]{:S(2)}) collective-permute-start(f32[512,128]{1,0:T(8,128)S(1)} %add.16.refs_8_), channel_id=1, source_target_pairs={{0,4},{1,5},{2,6},{3,7},{4,0},{5,1},{6,2},{7,3},{8,12},{9,13},{10,... | collective-permute-start | bytes 786440 | tf_op jit(solution)/shard_map/ppermute | solution.py:471
  70.7 0.8 collective-permute-start.29
  71.5 9.5 %collective-permute-done.15 = f32[512,128]{1,0:T(8,128)S(1)} collective-permute-done((f32[512,128]{1,0:T(8,128)}, f32[512,128]{1,0:T(8,128)S(1)}, u32[]{:S(2)}, u32[]{:S(2)}) %collective-permute-start.15) | collective-permute-done | bytes 262176 | tf_op jit(solution)/shard_map/ppermute | solution.py:471
  81.0 1.0 add.15.refs_8_
  82.0 1.3 %collective-permute-start.17 = (f32[512,128]{1,0:T(8,128)S(1)}, f32[512,128]{1,0:T(8,128)S(1)}, u32[]{:S(2)}, u32[]{:S(2)}) collective-permute-start(f32[512,128]{1,0:T(8,128)S(1)} %add.15.refs_8_), channel_id=1, source_target_pairs={{0,2},{1,3},{2,0},{3,1},{4,6},{5,7},{6,4},{7,5},{8,10},{9,11},{10,... | collective-permute-start | bytes 786440 | tf_op jit(solution)/shard_map/ppermute | solution.py:471
  83.3 0.7 collective-permute-done.27.refs_12_
  84.0 1.6 %collective-permute-start.21 = (f32[512,128]{1,0:T(8,128)S(1)}, f32[512,128]{1,0:T(8,128)S(1)}, u32[]{:S(2)}, u32[]{:S(2)}) collective-permute-start(f32[512,128]{1,0:T(8,128)S(1)} %add.15.refs_8_), channel_id=1, source_target_pairs={{0,6},{1,7},{2,4},{3,5},{4,2},{5,3},{6,0},{7,1},{8,14},{9,15},{10,... | collective-permute-start | bytes 786440 | tf_op jit(solution)/shard_map/ppermute | solution.py:471
  85.6 3.2 %collective-permute-done.29.refs_14_ = f32[512,128]{1,0:T(8,128)S(1)} collective-permute-done((f32[512,128]{1,0:T(8,128)S(1)}, f32[512,128]{1,0:T(8,128)S(1)}, u32[]{:S(2)}, u32[]{:S(2)}) %collective-permute-start.29) | collective-permute-done | bytes 262176 | tf_op jit(solution)/shard_map/ppermute | solution.py:471
  88.8 0.5 collective-permute-start.28
  89.3 5.0 %collective-permute-done.17.refs_10_ = f32[512,128]{1,0:T(8,128)S(1)} collective-permute-done((f32[512,128]{1,0:T(8,128)S(1)}, f32[512,128]{1,0:T(8,128)S(1)}, u32[]{:S(2)}, u32[]{:S(2)}) %collective-permute-start.17) | collective-permute-done | bytes 262176 | tf_op jit(solution)/shard_map/ppermute | solution.py:471
  94.3 0.9 collective-permute-done.19.refs_12_
  95.3 3.7 %collective-permute-done.21.refs_14_ = f32[512,128]{1,0:T(8,128)S(1)} collective-permute-done((f32[512,128]{1,0:T(8,128)S(1)}, f32[512,128]{1,0:T(8,128)S(1)}, u32[]{:S(2)}, u32[]{:S(2)}) %collective-permute-start.21) | collective-permute-done | bytes 262176 | tf_op jit(solution)/shard_map/ppermute | solution.py:471
  99.0 0.5 collective-permute-start.20
  99.6 0.6 copy-done.13
  100.2 0.7 copy-done.14
  100.9 3.1 %finish.2.refs_16_ = f32[8,4,128,128]{3,2,1,0:T(8,128)} custom-call(s32[1]{0:T(128)} %bitcast.own_ref, s32[16,32]{1,0:T(8,128)} %dest_ref.7, f32[8,128]{1,0:T(8,128)} %get-tuple-element.46.var_ref, f32[264,128]{1,0:T(8,128)} %get-tuple-element.37.refs_0_, f32[264,128]{1,0:T(8,128)} %get-tuple-element.38.refs_1_, f32[264,128]{1,0:T(8,128)} %get-tuple-element.39.refs_2_, ...), custom_call_target="tpu_custom_call" | custom-call | tf_op jit(solution)/shard_map/finish/pallas_call | solution.py:443
  104.1 0.6 copy-done.9
  105.0 3.1 %finish.3 = f32[8,4,128,128]{3,2,1,0:T(8,128)} custom-call(s32[1]{0:T(128)} %bitcast.own_ref, s32[16,32]{1,0:T(8,128)} %dest_ref.7, f32[8,128]{1,0:T(8,128)} %get-tuple-element.46.var_ref, f32[256,128]{1,0:T(8,128)} %get-tuple-element.28.refs_0_, f32[256,128]{1,0:T(8,128)} %get-tuple-element.29.refs_1_, ...), custom_call_target="tpu_custom_call", output_to_operand_aliasing={{}: (19, {})} | custom-call | tf_op jit(solution)/shard_map/finish/pallas_call | solution.py:443
  (83 shorter events, 0.9 us)
Async XLA Ops:
  7.8 5.9 %collective-permute-start.7 = (f32[8,128]{1,0:T(8,128)}, f32[8,128]{1,0:T(8,128)S(1)}, u32[]{:S(2)}, u32[]{:S(2)}) collective-permute-start(f32[8,128]{1,0:T(8,128)} %get-tuple-element.36.refs_0_), channel_id=1, source_target_pairs={{0,8},{1,9},{2,10},{3,11},{4,12},{5,13},{6,14},{7,15},{8,0},{9,1},... | collective-permute-start | bytes 12296 | tf_op jit(solution)/shard_map/ppermute | solution.py:471
  19.6 5.7 %collective-permute-start.10 = (f32[264,128]{1,0:T(8,128)}, f32[264,128]{1,0:T(8,128)S(1)}, u32[]{:S(2)}, u32[]{:S(2)}) collective-permute-start(f32[264,128]{1,0:T(8,128)} %get-tuple-element.40.refs_3_), channel_id=1, source_target_pairs={{0,3},{1,2},{2,1},{3,0},{4,7},{5,6},{6,5},{7,4},{8,11},{9,10},{10,... | collective-permute-start | bytes 405512 | tf_op jit(solution)/shard_map/ppermute | solution.py:471
  19.8 6.2 %collective-permute-start.11 = (f32[264,128]{1,0:T(8,128)}, f32[264,128]{1,0:T(8,128)S(1)}, u32[]{:S(2)}, u32[]{:S(2)}) collective-permute-start(f32[264,128]{1,0:T(8,128)} %get-tuple-element.41.refs_4_), channel_id=1, source_target_pairs={{0,4},{1,5},{2,6},{3,7},{4,0},{5,1},{6,2},{7,3},{8,12},{9,13},{10,... | collective-permute-start | bytes 405512 | tf_op jit(solution)/shard_map/ppermute | solution.py:471
  21.6 11.9 %collective-permute-start.12 = (f32[264,128]{1,0:T(8,128)}, f32[264,128]{1,0:T(8,128)S(1)}, u32[]{:S(2)}, u32[]{:S(2)}) collective-permute-start(f32[264,128]{1,0:T(8,128)} %get-tuple-element.42.refs_5_), channel_id=1, source_target_pairs={{0,5},{1,4},{2,7},{3,6},{4,1},{5,0},{6,3},{7,2},{8,13},{9,12},{10,... | collective-permute-start | bytes 405512 | tf_op jit(solution)/shard_map/ppermute | solution.py:471
  22.9 10.6 %collective-permute-start.13 = (f32[264,128]{1,0:T(8,128)}, f32[264,128]{1,0:T(8,128)S(1)}, u32[]{:S(2)}, u32[]{:S(2)}) collective-permute-start(f32[264,128]{1,0:T(8,128)} %get-tuple-element.43.refs_6_), channel_id=1, source_target_pairs={{0,6},{1,7},{2,4},{3,5},{4,2},{5,3},{6,0},{7,1},{8,14},{9,15},{10,... | collective-permute-start | bytes 405512 | tf_op jit(solution)/shard_map/ppermute | solution.py:471
  24.5 10.8 %collective-permute-start.14 = (f32[264,128]{1,0:T(8,128)}, f32[264,128]{1,0:T(8,128)S(1)}, u32[]{:S(2)}, u32[]{:S(2)}) collective-permute-start(f32[264,128]{1,0:T(8,128)} %get-tuple-element.44.refs_7_), channel_id=1, source_target_pairs={{0,7},{1,6},{2,5},{3,4},{4,3},{5,2},{6,1},{7,0},{8,15},{9,14},{10,... | collective-permute-start | bytes 405512 | tf_op jit(solution)/shard_map/ppermute | solution.py:471
  25.3 13.0 %copy-start.15 = (f32[264,128]{1,0:T(8,128)}, f32[264,128]{1,0:T(8,128)S(1)}, u32[]{:S(2)}) copy-start(f32[264,128]{1,0:T(8,128)S(1)} %collective-permute-done.10.refs_3_) | copy-start | bytes 405508
  25.3 10.9 %collective-permute-start.8 = (f32[264,128]{1,0:T(8,128)}, f32[264,128]{1,0:T(8,128)S(1)}, u32[]{:S(2)}, u32[]{:S(2)}) collective-permute-start(f32[264,128]{1,0:T(8,128)} %get-tuple-element.38.refs_1_), channel_id=1, source_target_pairs={{0,1},{1,0},{2,3},{3,2},{4,5},{5,4},{6,7},{7,6},{8,9},{9,8},{10,11... | collective-permute-start | bytes 405512 | tf_op jit(solution)/shard_map/ppermute | solution.py:471
  26.0 12.4 %copy-start.16 = (f32[264,128]{1,0:T(8,128)}, f32[264,128]{1,0:T(8,128)S(1)}, u32[]{:S(2)}) copy-start(f32[264,128]{1,0:T(8,128)S(1)} %collective-permute-done.11.refs_4_) | copy-start | bytes 405508
  26.0 12.4 %collective-permute-start.9 = (f32[264,128]{1,0:T(8,128)}, f32[264,128]{1,0:T(8,128)S(1)}, u32[]{:S(2)}, u32[]{:S(2)}) collective-permute-start(f32[264,128]{1,0:T(8,128)} %get-tuple-element.39.refs_2_), channel_id=1, source_target_pairs={{0,2},{1,3},{2,0},{3,1},{4,6},{5,7},{6,4},{7,5},{8,10},{9,11},{10,... | collective-permute-start | bytes 405512 | tf_op jit(solution)/shard_map/ppermute | solution.py:471
  33.5 4.9 %copy-start.17 = (f32[264,128]{1,0:T(8,128)}, f32[264,128]{1,0:T(8,128)S(1)}, u32[]{:S(2)}) copy-start(f32[264,128]{1,0:T(8,128)S(1)} %collective-permute-done.12.refs_5_) | copy-start | bytes 405508
  33.5 12.6 %collective-permute-start = (f32[256,128]{1,0:T(8,128)}, f32[256,128]{1,0:T(8,128)S(1)}, u32[]{:S(2)}, u32[]{:S(2)}) collective-permute-start(f32[256,128]{1,0:T(8,128)} %get-tuple-element.29.refs_1_), channel_id=1, source_target_pairs={{0,1},{1,0},{2,3},{3,2},{4,5},{5,4},{6,7},{7,6},{8,9},{9,8},{10,11... | collective-permute-start | bytes 393224 | tf_op jit(solution)/shard_map/ppermute | solution.py:471
  33.6 12.5 %collective-permute-start.1 = (f32[256,128]{1,0:T(8,128)}, f32[256,128]{1,0:T(8,128)S(1)}, u32[]{:S(2)}, u32[]{:S(2)}) collective-permute-start(f32[256,128]{1,0:T(8,128)} %get-tuple-element.30.refs_2_), channel_id=1, source_target_pairs={{0,2},{1,3},{2,0},{3,1},{4,6},{5,7},{6,4},{7,5},{8,10},{9,11},{10,... | collective-permute-start | bytes 393224 | tf_op jit(solution)/shard_map/ppermute | solution.py:471
  35.3 12.1 %collective-permute-start.2 = (f32[256,128]{1,0:T(8,128)}, f32[256,128]{1,0:T(8,128)S(1)}, u32[]{:S(2)}, u32[]{:S(2)}) collective-permute-start(f32[256,128]{1,0:T(8,128)} %get-tuple-element.31.refs_3_), channel_id=1, source_target_pairs={{0,3},{1,2},{2,1},{3,0},{4,7},{5,6},{6,5},{7,4},{8,11},{9,10},{10,... | collective-permute-start | bytes 393224 | tf_op jit(solution)/shard_map/ppermute | solution.py:471
  41.8 25.2 %collective-permute-start.23 = (f32[512,128]{1,0:T(8,128)}, f32[512,128]{1,0:T(8,128)S(1)}, u32[]{:S(2)}, u32[]{:S(2)}) collective-permute-start(f32[512,128]{1,0:T(8,128)} %get-tuple-element.48), channel_id=1, source_target_pairs={{0,8},{1,9},{2,10},{3,11},{4,12},{5,13},{6,14},{7,15},{8,0},{9,1},... | collective-permute-start | bytes 786440 | tf_op jit(solution)/shard_map/ppermute | solution.py:471
  44.6 9.9 %collective-permute-start.3 = (f32[256,128]{1,0:T(8,128)}, f32[256,128]{1,0:T(8,128)S(1)}, u32[]{:S(2)}, u32[]{:S(2)}) collective-permute-start(f32[256,128]{1,0:T(8,128)} %get-tuple-element.32.refs_4_), channel_id=1, source_target_pairs={{0,4},{1,5},{2,6},{3,7},{4,0},{5,1},{6,2},{7,3},{8,12},{9,13},{10,... | collective-permute-start | bytes 393224 | tf_op jit(solution)/shard_map/ppermute | solution.py:471
  46.1 16.4 %copy-start.22 = (f32[256,128]{1,0:T(8,128)}, f32[256,128]{1,0:T(8,128)S(1)}, u32[]{:S(2)}) copy-start(f32[256,128]{1,0:T(8,128)S(1)} %collective-permute-done.refs_1_) | copy-start | bytes 393220
  46.1 11.1 %collective-permute-start.4 = (f32[256,128]{1,0:T(8,128)}, f32[256,128]{1,0:T(8,128)S(1)}, u32[]{:S(2)}, u32[]{:S(2)}) collective-permute-start(f32[256,128]{1,0:T(8,128)} %get-tuple-element.33.refs_5_), channel_id=1, source_target_pairs={{0,5},{1,4},{2,7},{3,6},{4,1},{5,0},{6,3},{7,2},{8,13},{9,12},{10,... | collective-permute-start | bytes 393224 | tf_op jit(solution)/shard_map/ppermute | solution.py:471
  46.1 16.4 %copy-start.23 = (f32[256,128]{1,0:T(8,128)}, f32[256,128]{1,0:T(8,128)S(1)}, u32[]{:S(2)}) copy-start(f32[256,128]{1,0:T(8,128)S(1)} %collective-permute-done.1.refs_2_) | copy-start | bytes 393220
  46.2 15.3 %collective-permute-start.5 = (f32[256,128]{1,0:T(8,128)}, f32[256,128]{1,0:T(8,128)S(1)}, u32[]{:S(2)}, u32[]{:S(2)}) collective-permute-start(f32[256,128]{1,0:T(8,128)} %get-tuple-element.34.refs_6_), channel_id=1, source_target_pairs={{0,6},{1,7},{2,4},{3,5},{4,2},{5,3},{6,0},{7,1},{8,14},{9,15},{10,... | collective-permute-start | bytes 393224 | tf_op jit(solution)/shard_map/ppermute | solution.py:471
  47.4 15.1 %copy-start.24 = (f32[256,128]{1,0:T(8,128)}, f32[256,128]{1,0:T(8,128)S(1)}, u32[]{:S(2)}) copy-start(f32[256,128]{1,0:T(8,128)S(1)} %collective-permute-done.2.refs_3_) | copy-start | bytes 393220
  47.4 15.1 %collective-permute-start.6 = (f32[256,128]{1,0:T(8,128)}, f32[256,128]{1,0:T(8,128)S(1)}, u32[]{:S(2)}, u32[]{:S(2)}) collective-permute-start(f32[256,128]{1,0:T(8,128)} %get-tuple-element.35.refs_7_), channel_id=1, source_target_pairs={{0,7},{1,6},{2,5},{3,4},{4,3},{5,2},{6,1},{7,0},{8,15},{9,14},{10,... | collective-permute-start | bytes 393224 | tf_op jit(solution)/shard_map/ppermute | solution.py:471
  54.4 8.1 %copy-start.25 = (f32[256,128]{1,0:T(8,128)}, f32[256,128]{1,0:T(8,128)S(1)}, u32[]{:S(2)}) copy-start(f32[256,128]{1,0:T(8,128)S(1)} %collective-permute-done.3.refs_4_) | copy-start | bytes 393220
  57.2 5.3 %copy-start.26 = (f32[256,128]{1,0:T(8,128)}, f32[256,128]{1,0:T(8,128)S(1)}, u32[]{:S(2)}) copy-start(f32[256,128]{1,0:T(8,128)S(1)} %collective-permute-done.4.refs_5_) | copy-start | bytes 393220
  66.0 15.1 %collective-permute-start.15 = (f32[512,128]{1,0:T(8,128)}, f32[512,128]{1,0:T(8,128)S(1)}, u32[]{:S(2)}, u32[]{:S(2)}) collective-permute-start(f32[512,128]{1,0:T(8,128)} %get-tuple-element.47), channel_id=1, source_target_pairs={{0,8},{1,9},{2,10},{3,11},{4,12},{5,13},{6,14},{7,15},{8,0},{9,1},... | collective-permute-start | bytes 786440 | tf_op jit(solution)/shard_map/ppermute | solution.py:471
  68.0 32.9 %copy-start.1 = (f32[512,128]{1,0:T(8,128)}, f32[512,128]{1,0:T(8,128)S(1)}, u32[]{:S(2)}) copy-start(f32[512,128]{1,0:T(8,128)S(1)} %add.16.refs_8_) | copy-start | bytes 786436
  68.0 15.3 %collective-permute-start.25 = (f32[512,128]{1,0:T(8,128)S(1)}, f32[512,128]{1,0:T(8,128)S(1)}, u32[]{:S(2)}, u32[]{:S(2)}) collective-permute-start(f32[512,128]{1,0:T(8,128)S(1)} %add.16.refs_8_), channel_id=1, source_target_pairs={{0,2},{1,3},{2,0},{3,1},{4,6},{5,7},{6,4},{7,5},{8,10},{9,11},{10,... | collective-permute-start | bytes 786440 | tf_op jit(solution)/shard_map/ppermute | solution.py:471
  69.3 14.7 %collective-permute-start.27 = (f32[512,128]{1,0:T(8,128)S(1)}, f32[512,128]{1,0:T(8,128)S(1)}, u32[]{:S(2)}, u32[]{:S(2)}) collective-permute-start(f32[512,128]{1,0:T(8,128)S(1)} %add.16.refs_8_), channel_id=1, source_target_pairs={{0,4},{1,5},{2,6},{3,7},{4,0},{5,1},{6,2},{7,3},{8,12},{9,13},{10,... | collective-permute-start | bytes 786440 | tf_op jit(solution)/shard_map/ppermute | solution.py:471
  70.7 18.0 %collective-permute-start.29 = (f32[512,128]{1,0:T(8,128)S(1)}, f32[512,128]{1,0:T(8,128)S(1)}, u32[]{:S(2)}, u32[]{:S(2)}) collective-permute-start(f32[512,128]{1,0:T(8,128)S(1)} %add.16.refs_8_), channel_id=1, source_target_pairs={{0,6},{1,7},{2,4},{3,5},{4,2},{5,3},{6,0},{7,1},{8,14},{9,15},{10,... | collective-permute-start | bytes 786440 | tf_op jit(solution)/shard_map/ppermute | solution.py:471
  71.5 17.3 %collective-permute-start.24 = (f32[512,128]{1,0:T(8,128)S(1)}, f32[512,128]{1,0:T(8,128)S(1)}, u32[]{:S(2)}, u32[]{:S(2)}) collective-permute-start(f32[512,128]{1,0:T(8,128)S(1)} %add.16.refs_8_), channel_id=1, source_target_pairs={{0,1},{1,0},{2,3},{3,2},{4,5},{5,4},{6,7},{7,6},{8,9},{9,8},{10,11... | collective-permute-start | bytes 786440 | tf_op jit(solution)/shard_map/ppermute | solution.py:471
  82.0 22.0 %copy-start = (f32[512,128]{1,0:T(8,128)}, f32[512,128]{1,0:T(8,128)S(1)}, u32[]{:S(2)}) copy-start(f32[512,128]{1,0:T(8,128)S(1)} %add.15.refs_8_) | copy-start | bytes 786436
  82.0 12.3 %collective-permute-start.17 = (f32[512,128]{1,0:T(8,128)S(1)}, f32[512,128]{1,0:T(8,128)S(1)}, u32[]{:S(2)}, u32[]{:S(2)}) collective-permute-start(f32[512,128]{1,0:T(8,128)S(1)} %add.15.refs_8_), channel_id=1, source_target_pairs={{0,2},{1,3},{2,0},{3,1},{4,6},{5,7},{6,4},{7,5},{8,10},{9,11},{10,... | collective-permute-start | bytes 786440 | tf_op jit(solution)/shard_map/ppermute | solution.py:471
  83.3 17.6 %copy-start.4 = (f32[512,128]{1,0:T(8,128)}, f32[512,128]{1,0:T(8,128)S(1)}, u32[]{:S(2)}) copy-start(f32[512,128]{1,0:T(8,128)S(1)} %collective-permute-done.25.refs_10_) | copy-start | bytes 786436
  83.3 12.0 %collective-permute-start.19 = (f32[512,128]{1,0:T(8,128)S(1)}, f32[512,128]{1,0:T(8,128)S(1)}, u32[]{:S(2)}, u32[]{:S(2)}) collective-permute-start(f32[512,128]{1,0:T(8,128)S(1)} %add.15.refs_8_), channel_id=1, source_target_pairs={{0,4},{1,5},{2,6},{3,7},{4,0},{5,1},{6,2},{7,3},{8,12},{9,13},{10,... | collective-permute-start | bytes 786440 | tf_op jit(solution)/shard_map/ppermute | solution.py:471
  84.0 16.9 %copy-start.5 = (f32[512,128]{1,0:T(8,128)}, f32[512,128]{1,0:T(8,128)S(1)}, u32[]{:S(2)}) copy-start(f32[512,128]{1,0:T(8,128)S(1)} %collective-permute-done.27.refs_12_) | copy-start | bytes 786436
  84.0 15.0 %collective-permute-start.21 = (f32[512,128]{1,0:T(8,128)S(1)}, f32[512,128]{1,0:T(8,128)S(1)}, u32[]{:S(2)}, u32[]{:S(2)}) collective-permute-start(f32[512,128]{1,0:T(8,128)S(1)} %add.15.refs_8_), channel_id=1, source_target_pairs={{0,6},{1,7},{2,4},{3,5},{4,2},{5,3},{6,0},{7,1},{8,14},{9,15},{10,... | collective-permute-start | bytes 786440 | tf_op jit(solution)/shard_map/ppermute | solution.py:471
  88.8 12.1 %copy-start.7 = (f32[512,128]{1,0:T(8,128)}, f32[512,128]{1,0:T(8,128)S(1)}, u32[]{:S(2)}) copy-start(f32[512,128]{1,0:T(8,128)S(1)} %collective-permute-done.29.refs_14_) | copy-start | bytes 786436
  88.8 10.2 %collective-permute-start.26 = (f32[512,128]{1,0:T(8,128)S(1)}, f32[512,128]{1,0:T(8,128)S(1)}, u32[]{:S(2)}, u32[]{:S(2)}) collective-permute-start(f32[512,128]{1,0:T(8,128)S(1)} %collective-permute-done.25.refs_10_), channel_id=1, source_target_pairs={{0,1},{1,0},{2,3},{3,2},{4,5},{5,4},{6,7},{7,6},{8,9},{9,8},{10,11... | collective-permute-start | bytes 786440 | tf_op jit(solution)/shard_map/ppermute | solution.py:471
  88.8 12.1 %copy-start.8 = (f32[512,128]{1,0:T(8,128)}, f32[512,128]{1,0:T(8,128)S(1)}, u32[]{:S(2)}) copy-start(f32[512,128]{1,0:T(8,128)S(1)} %collective-permute-done.24.refs_9_) | copy-start | bytes 786436
  88.8 10.7 %collective-permute-start.28 = (f32[512,128]{1,0:T(8,128)S(1)}, f32[512,128]{1,0:T(8,128)S(1)}, u32[]{:S(2)}, u32[]{:S(2)}) collective-permute-start(f32[512,128]{1,0:T(8,128)S(1)} %collective-permute-done.27.refs_12_), channel_id=1, source_target_pairs={{0,1},{1,0},{2,3},{3,2},{4,5},{5,4},{6,7},{7,6},{8,9},{9,8},{10,11... | collective-permute-start | bytes 786440 | tf_op jit(solution)/shard_map/ppermute | solution.py:471
  94.3 9.7 %copy-start.2 = (f32[512,128]{1,0:T(8,128)}, f32[512,128]{1,0:T(8,128)S(1)}, u32[]{:S(2)}) copy-start(f32[512,128]{1,0:T(8,128)S(1)} %collective-permute-done.17.refs_10_) | copy-start | bytes 786436
  94.3 9.8 %collective-permute-start.16 = (f32[512,128]{1,0:T(8,128)S(1)}, f32[512,128]{1,0:T(8,128)S(1)}, u32[]{:S(2)}, u32[]{:S(2)}) collective-permute-start(f32[512,128]{1,0:T(8,128)S(1)} %add.15.refs_8_), channel_id=1, source_target_pairs={{0,1},{1,0},{2,3},{3,2},{4,5},{5,4},{6,7},{7,6},{8,9},{9,8},{10,11... | collective-permute-start | bytes 786440 | tf_op jit(solution)/shard_map/ppermute | solution.py:471
  95.2 8.8 %copy-start.3 = (f32[512,128]{1,0:T(8,128)}, f32[512,128]{1,0:T(8,128)S(1)}, u32[]{:S(2)}) copy-start(f32[512,128]{1,0:T(8,128)S(1)} %collective-permute-done.19.refs_12_) | copy-start | bytes 786436
  95.2 4.3 %collective-permute-start.30 = (f32[512,128]{1,0:T(8,128)S(1)}, f32[512,128]{1,0:T(8,128)S(1)}, u32[]{:S(2)}, u32[]{:S(2)}) collective-permute-start(f32[512,128]{1,0:T(8,128)S(1)} %collective-permute-done.29.refs_14_), channel_id=1, source_target_pairs={{0,1},{1,0},{2,3},{3,2},{4,5},{5,4},{6,7},{7,6},{8,9},{9,8},{10,11... | collective-permute-start | bytes 786440 | tf_op jit(solution)/shard_map/ppermute | solution.py:471
  99.0 5.1 %copy-start.6 = (f32[512,128]{1,0:T(8,128)}, f32[512,128]{1,0:T(8,128)S(1)}, u32[]{:S(2)}) copy-start(f32[512,128]{1,0:T(8,128)S(1)} %collective-permute-done.21.refs_14_) | copy-start | bytes 786436
  99.0 5.1 %collective-permute-start.18 = (f32[512,128]{1,0:T(8,128)S(1)}, f32[512,128]{1,0:T(8,128)S(1)}, u32[]{:S(2)}, u32[]{:S(2)}) collective-permute-start(f32[512,128]{1,0:T(8,128)S(1)} %collective-permute-done.17.refs_10_), channel_id=1, source_target_pairs={{0,1},{1,0},{2,3},{3,2},{4,5},{5,4},{6,7},{7,6},{8,9},{9,8},{10,11... | collective-permute-start | bytes 786440 | tf_op jit(solution)/shard_map/ppermute | solution.py:471
  99.0 5.1 %collective-permute-start.20 = (f32[512,128]{1,0:T(8,128)S(1)}, f32[512,128]{1,0:T(8,128)S(1)}, u32[]{:S(2)}, u32[]{:S(2)}) collective-permute-start(f32[512,128]{1,0:T(8,128)S(1)} %collective-permute-done.19.refs_12_), channel_id=1, source_target_pairs={{0,1},{1,0},{2,3},{3,2},{4,5},{5,4},{6,7},{7,6},{8,9},{9,8},{10,11... | collective-permute-start | bytes 786440 | tf_op jit(solution)/shard_map/ppermute | solution.py:471
  99.5 4.6 %collective-permute-start.22 = (f32[512,128]{1,0:T(8,128)S(1)}, f32[512,128]{1,0:T(8,128)}, u32[]{:S(2)}, u32[]{:S(2)}) collective-permute-start(f32[512,128]{1,0:T(8,128)S(1)} %collective-permute-done.21.refs_14_), channel_id=1, source_target_pairs={{0,1},{1,0},{2,3},{3,2},{4,5},{5,4},{6,7},{7,6},{8,9},{9,8},{10,11... | collective-permute-start | bytes 786440 | tf_op jit(solution)/shard_map/ppermute | solution.py:471
  (13 other events, 18.8 us)

commit v2 on v1

--- a/solution.py
+++ b/solution.py
@@ -56,23 +56,6 @@
 def sinc(x):
     angle = jnp.where(x == 0, 1.0, jnp.pi * x)
     return jnp.where(x == 0, 1.0, jnp.sin(angle) / angle)
-
-
-def banded_region(tap_row, rows, width, taps, first, offset, span):
-    lane, diff = iotas(8)
-    wide = jnp.broadcast_to(tap_row, (8, LANES))
-    chunks = []
-    for start in range(0, rows, 8):
-        lead = start + first + offset
-        rolled = skew(wide, lead)
-        cols = []
-        for tile in range(width // LANES):
-            begin = LANES * tile
-            k = diff + (begin - lead)
-            keep = (k >= 0) & (k < taps) & (lane >= offset - begin) & (lane < offset + span - begin)
-            cols.append(jnp.where(keep, rolled, 0.0))
-        chunks.append(jnp.concatenate(cols, axis=1))
-    return jnp.concatenate(chunks, axis=0)
 
 
 def fill_matched_coefficients(step, table, h_win, side, filters, taps, length, win):
@@ -248,78 +231,78 @@
     )(images, coeffs, row_taps, col_taps)
 
 
-def warp_kernel(own_ref, sub_ref, m_ref, *refs, strips, part, parts, pack, powers):
+def warp_kernel(own_ref, sub_ref, m_ref, *refs, strips, parts, pack, powers):
     given = refs[:powers]
-    outs = refs[powers : powers + strips]
-    shifts, held = refs[powers + strips :]
+    outs = refs[powers : powers + strips * parts]
+    shifts, held, totals, sems = refs[powers + strips * parts :]
     step = pl.program_id(0)
     half = m_ref.shape[1] // 2
-    rows = half // parts
-    height = rows // strips
-    low = max(part * rows - 3, 0) // 16 * 16
-    span = min(-(-(part * rows + rows + 2) // 16) * 16, half) - low
-    depth = -(-3 * span // LANES) * LANES
+    height = half // strips // parts
+    fetches = [
+        pltpu.make_async_copy(given[i], totals.at[i], sems.at[i]) for i in range(powers)
+    ]
 
     @pl.when(step == 0)
     def _():
+        for fetch in fetches:
+            fetch.start()
         lanes = lax.broadcasted_iota(jnp.int32, (1, LANES), 1).astype(jnp.float32)
         for axis, steps in enumerate((2.0 - lanes, lanes - 3.0)):
             distance = steps + as_column(sub_ref[axis : axis + 1, :])
             value = sinc(distance) * sinc(distance / 3.0)
             shifts[axis] = jnp.where(jnp.abs(distance) < 3.0, value, 0.0)
 
-    lane = lax.broadcasted_iota(jnp.int32, (1, depth), 1)
     for n in range(pack):
         image = step * pack + n
-        left = jnp.zeros((rows, depth), jnp.float32)
-        for copy in range(3):
-            left += banded_region(
-                shifts[0, pl.ds(image, 1), :], rows, depth, 6, part * rows - low - 2, copy * span, span
-            )
-        high = left.astype(jnp.bfloat16).astype(jnp.float32)
-        left = jnp.where(lane < 2 * span, high, left - high).astype(jnp.bfloat16)
+        vertical = split(banded_rows(shifts[0, pl.ds(image, 1), :], half, 6, -2))
         horizontal = split(banded_rows(shifts[1, pl.ds(image, 1), :], half, 6, -3))
+        left = jnp.concatenate([vertical[0], vertical[0], vertical[1]], axis=1)
         right = jnp.concatenate([horizontal[0], horizontal[0], horizontal[1]], axis=0)
         moved = []
         for side in range(2):
-            upper, lower = split(m_ref[n, side * half + low : side * half + low + span, :])
-            stacked = [upper, lower, upper]
-            if depth > 3 * span:
-                stacked.append(jnp.zeros((depth - 3 * span, 2 * half), jnp.bfloat16))
+            upper, lower = split(m_ref[n, side * half : (side + 1) * half, :])
             full = jnp.dot(
-                left, jnp.concatenate(stacked, axis=0), preferred_element_type=jnp.float32
+                left,
+                jnp.concatenate([upper, lower, upper], axis=0),
+                preferred_element_type=jnp.float32,
             )
             moved += [full[:, :half], full[:, half:]]
         upper, lower = split(jnp.concatenate(moved, axis=0))
         lhs = jnp.concatenate([upper, lower, upper], axis=1)
-        held[n] = jnp.dot(lhs, right, preferred_element_type=jnp.float32).reshape(4, rows, half)
+        held[n] = jnp.dot(lhs, right, preferred_element_type=jnp.float32).reshape(4, half, half)
     for n in range(pack):
-        for k in range(strips):
-            begin = pl.ds(pl.multiple_of((own_ref[0] ^ k) * height, height), height)
-            for block in range(4):
-                item = 4 * (step * pack + n) + block
-                at = pl.ds(pl.multiple_of(item * height, height), height)
-                outs[k][at, :] = held[n, block, begin, :]
-
-    if powers:
-
-        @pl.when(step == pl.num_programs(0) - 1)
-        def _():
-            total = given[0][...]
-            for other in given[1:]:
-                total = total + other[...]
-            for out in outs:
-                out[out.shape[0] - total.shape[0] :, :] = total
-
-
-def warp(own, subpixel, matched, powers, part, parts, strips):
+        for part in range(parts):
+            for k in range(strips):
+                begin = (part * strips + (own_ref[0] ^ k)) * height
+                rows = pl.ds(pl.multiple_of(begin, height), height)
+                for block in range(4):
+                    item = 4 * (step * pack + n) + block
+                    at = pl.ds(pl.multiple_of(item * height, height), height)
+                    outs[part * strips + k][at, :] = held[n, block, rows, :]
+
+    @pl.when(step == pl.num_programs(0) - 1)
+    def _():
+        for fetch in fetches:
+            fetch.wait()
+        total = jnp.sum(totals[...], axis=0)
+        for out in outs[:strips]:
+            out[out.shape[0] - total.shape[0] :, :] = total
+
+
+def warp(own, subpixel, matched, powers, parts, strips):
     count, length, _ = matched.shape
     half = length // 2
-    rows = count * 4 * half // strips // parts + sum(p.shape[0] for p in powers[:1])
+    rows = count * 4 * half // strips // parts
+    pow_rows = powers[0].shape[0]
     pack = 2 - count % 2
-    return pl.pallas_call(
+    shapes = [
+        jax.ShapeDtypeStruct((rows + (0 if part else pow_rows), half), jnp.float32)
+        for part in range(parts)
+        for _ in range(strips)
+    ]
+    outs = pl.pallas_call(
         functools.partial(
-            warp_kernel, strips=strips, part=part, parts=parts, pack=pack, powers=len(powers)
+            warp_kernel, strips=strips, parts=parts, pack=pack, powers=len(powers)
         ),
         grid_spec=pltpu.PrefetchScalarGridSpec(
             num_scalar_prefetch=1,
@@ -328,16 +311,19 @@
                 pl.BlockSpec(subpixel.shape, lambda i, own: (0, 0)),
                 pl.BlockSpec((pack, length, length), lambda i, own: (i, 0, 0)),
             ]
-            + [pl.BlockSpec(p.shape, lambda i, own: (0, 0)) for p in powers],
-            out_specs=[pl.BlockSpec((rows, half), lambda i, own: (0, 0))] * strips,
+            + [pl.BlockSpec(memory_space=pltpu.HBM)] * len(powers),
+            out_specs=[pl.BlockSpec(x.shape, lambda i, own: (0, 0)) for x in shapes],
             scratch_shapes=[
                 pltpu.VMEM((2, count, LANES), jnp.float32),
-                pltpu.VMEM((pack, 4, half // parts, half), jnp.float32),
+                pltpu.VMEM((pack, 4, half, half), jnp.float32),
+                pltpu.VMEM((len(powers), pow_rows, LANES), jnp.float32),
+                pltpu.SemaphoreType.DMA((len(powers),)),
             ],
         ),
-        out_shape=[jax.ShapeDtypeStruct((rows, half), jnp.float32)] * strips,
+        out_shape=shapes,
         name="warp",
     )(own, subpixel, matched, *powers)
+    return [outs[part * strips : (part + 1) * strips] for part in range(parts)]
 
 
 def reduce_kernel(own_ref, dest_ref, slot_ref, *refs, strips, slots, images, visits, pixels):
@@ -415,39 +401,58 @@
     )(own, dest, dest, *pieces, *given)
 
 
-def finish_kernel(own_ref, dest_ref, var_ref, *refs, strips, visits):
-    warped = refs[:strips]
-    templates = refs[strips : 2 * strips]
-    out_ref = refs[-1]
+def finish_kernel(own_ref, dest_ref, var_ref, *refs, groups, visits, aliased):
+    count = 2 * len(groups)
+    warped = refs[:count]
+    templates = refs[count : 2 * count]
+    out_ref, held, sems = refs[2 * count + aliased :]
     own = own_ref[0]
-    height = out_ref.shape[2] // strips
+    images = out_ref.shape[0]
+    height = held.shape[3] // 2
     inverse = 1.0 / jnp.sqrt(var_ref[...])
-    for image in range(out_ref.shape[0]):
-        visit = image % visits
-        scale = jnp.broadcast_to(inverse[visit : visit + 1, :], (height, LANES))
-        for block in range(4):
-            item = 4 * image + block
-            at = pl.ds(pl.multiple_of(dest_ref[own, item] * height, height), height)
-            for k in range(strips):
-                here = warped[k][item * height : (item + 1) * height, :]
-                rows = pl.ds(pl.multiple_of(((own % strips) ^ k) * height, height), height)
-                out_ref[image, block, rows, :] = (here - templates[k][at, :]) * scale
-
-
-def finish(own, dest, variance, warped, templates, previous, part, images, visits):
-    strips = len(warped)
+    copies = []
+    for g, (pair, part) in enumerate(groups):
+        for image in range(images):
+            visit = image % visits
+            scale = jnp.broadcast_to(inverse[visit : visit + 1, :], (height, LANES))
+            for block in range(4):
+                item = 4 * image + block
+                at = pl.ds(pl.multiple_of(dest_ref[own, item] * height, height), height)
+                for k in range(2):
+                    here = warped[2 * g + k][item * height : (item + 1) * height, :]
+                    rows = pl.ds(pl.multiple_of(((own & 1) ^ k) * height, height), height)
+                    held[g, image, block, rows, :] = (here - templates[2 * g + k][at, :]) * scale
+        strip = (own % GROUP // 2) ^ (pair // 2)
+        begin = pl.multiple_of((part * GROUP + 2 * strip) * height, 2 * height)
+        copies.append(
+            pltpu.make_async_copy(
+                held.at[g], out_ref.at[:, :, pl.ds(begin, 2 * height), :], sems.at[g]
+            )
+        )
+        copies[-1].start()
+    for copy in copies:
+        copy.wait()
+
+
+def finish(own, dest, variance, warped, full, previous, groups, images, visits):
+    keys = [(part, k) for pair, part in groups for k in (pair, pair + 1)]
+    mine = [warped[part][k] for part, k in keys]
+    templates = [full[part][k] for part, k in keys]
+    height = BLOCK // GROUP // PARTS
     smem = pl.BlockSpec(memory_space=pltpu.SMEM)
     vmem = pl.BlockSpec(memory_space=pltpu.VMEM)
+    hbm = pl.BlockSpec(memory_space=pl.ANY)
     extra = [] if previous is None else [previous]
-    inputs = [variance, *warped, *templates]
+    inputs = [variance, *mine, *templates]
     return pl.pallas_call(
-        functools.partial(finish_kernel, strips=strips, visits=visits),
-        grid=(1,),
-        in_specs=[smem, smem]
-        + [vmem] * len(inputs)
-        + [pl.BlockSpec(memory_space=pl.ANY) for _ in extra],
-        out_specs=pl.BlockSpec((images, 4, BLOCK // PARTS, LANES), lambda i: (0, 0, part, 0)),
+        functools.partial(finish_kernel, groups=groups, visits=visits, aliased=len(extra)),
+        in_specs=[smem, smem] + [vmem] * len(inputs) + [hbm] * len(extra),
+        out_specs=hbm,
         out_shape=jax.ShapeDtypeStruct((images, 4, BLOCK, LANES), jnp.float32),
+        scratch_shapes=[
+            pltpu.VMEM((len(groups), images, 4, 2 * height, LANES), jnp.float32),
+            pltpu.SemaphoreType.DMA((len(groups),)),
+        ],
         input_output_aliases={2 + len(inputs): 0} if extra else {},
         name="finish",
     )(own, dest, *inputs, *extra)
@@ -486,13 +491,10 @@
     )
     powers = [power] + [ahead(power, r) for r in range(1, others)]
     shifts = subpixel.transpose(2, 0, 1).reshape(2, images)
-    warped = []
+    warped = warp(own % GROUP, shifts, matched, powers, PARTS, GROUP)
     pieces = []
     for part in range(PARTS):
-        mine = warp(
-            own % GROUP, shifts, matched, [] if part else powers, part, PARTS, GROUP
-        )
-        warped.append(mine)
+        mine = warped[part]
         pieces.append([mine[0]] + [swap(mine[k], k) for k in range(1, GROUP)])
     full = []
     variance = None
@@ -506,16 +508,19 @@
             template = template + piece
         two = swap(template, 2)
         four = swap(template, 4)
-        six = swap(template, 6)
+        six = swap(two, 4) if part == 0 else swap(four, 2)
         full.append(
             [template, swap(template, 1)]
             + [two, swap(two, 1)]
             + [four, swap(four, 1)]
             + [six, swap(six, 1)]
         )
+    last = GROUP - 2
+    early = tuple((pair, part) for part in range(PARTS) for pair in range(0, last, 2))
+    late = tuple((last, part) for part in range(PARTS))
     result = None
-    for part in range(PARTS):
-        result = finish(own, dest, variance, warped[part], full[part], result, part, images, visits)
+    for groups in (early, late):
+        result = finish(own, dest, variance, warped, full, result, groups, images, visits)
     return result.reshape(tile_count, visits, 4, BLOCK, BLOCK)
 
 

time: 108 us -> 103 us (0.954)
  the two profiles are of different devices: /device:TPU:0 before, /device:TPU:1 now
where the time goes in v2:
time: 103 us
  starting transfers between devices  38.3 us (37%)
  waiting for transfers between devices  34 us (33%)
  Pallas kernels  26 us (25%)
  local copies, waits for them, and re-layouts  2.04 us (2%)
  other arithmetic  1.98 us (2%)
    ppermute x31, starting transfers between devices, permute(): return lax.ppermute(x, 'tile', [(i, target(i)) for i in range(devices)])  38.3 us
    ppermute x31, waiting for transfers between devices, permute(): return lax.ppermute(x, 'tile', [(i, target(i)) for i in range(devices)])  34 us
    pallas_call x1, Pallas kernels, match(): pl.pallas_call(functools.partial(match_kernel, pack=pack, visits=visits),...  7.79 us
    pallas_call x1, Pallas kernels, warp(): pl.pallas_call(functools.partial(warp_kernel, strips=strips, parts=parts,...  6.47 us
    pallas_call x2, Pallas kernels, finish(): pl.pallas_call(functools.partial(finish_kernel, groups=groups, visits=vis...  6.21 us
    pallas_call x2, Pallas kernels, reduce_blocks(): pl.pallas_call(kernel, in_specs=[smem, smem] + [vmem] * (1 + len(pieces)...  5.56 us
  transfers between devices with their start and end apart: 31, of which 13 were waited for; matrix products, arithmetic and copies ran while one was open for 2% of the time, Pallas kernels for 6%

profile of v2, /device:TPU:1, one launch (start us, length us, event | category | flops | bytes accessed | tf_op | source)
XLA Modules:
  0.0 102.7 jit_solution(16065360070549041346)
XLA Ops:
  0.0 7.8 %match.1 = (f32[8,256,256]{2,1,0:T(8,128)}, f32[8,128]{1,0:T(8,128)}) custom-call(f32[8,256,256]{2,1,0:T(8,128)} %bitcast.9, f32[6,8,25]{2,1,0:T(8,128)} %bitcast.10, bf16[5,21]{1,0:T(8,128)(2,1)} %rtap_ref.1, bf16[5,21]{1,0:T(8,128)(2,1)} %ctap_ref.1), custom_call_target="tpu_custom_call" | custom-call | tf_op jit(solution)/shard_map/match/pallas_call | solution.py:205
  7.8 3.1 %collective-permute-start = (f32[8,128]{1,0:T(8,128)}, f32[8,128]{1,0:T(8,128)S(1)}, u32[]{:S(2)}, u32[]{:S(2)}) collective-permute-start(f32[8,128]{1,0:T(8,128)} %get-tuple-element.28.refs_0_), channel_id=1, source_target_pairs={{0,8},{1,9},{2,10},{3,11},{4,12},{5,13},{6,14},{7,15},{8,0},{9,1},... | collective-permute-start | bytes 12296 | tf_op jit(solution)/shard_map/ppermute | solution.py:476
  10.9 1.2 %collective-permute-done.refs_1_ = f32[8,128]{1,0:T(8,128)S(1)} collective-permute-done((f32[8,128]{1,0:T(8,128)}, f32[8,128]{1,0:T(8,128)S(1)}, u32[]{:S(2)}, u32[]{:S(2)}) %collective-permute-start) | collective-permute-done | bytes 4128 | tf_op jit(solution)/shard_map/ppermute | solution.py:476
  12.1 0.6 copy-done.27
  12.7 6.5 %warp.1 = (f32[264,128]{1,0:T(8,128)}, f32[264,128]{1,0:T(8,128)}, f32[264,128]{1,0:T(8,128)}, f32[264,128]{1,0:T(8,128)}, f32[264,128]{1,0:T(8,128)}, /*index=5...) custom-call(s32[1]{0:T(128)S(6)} %select_n.7.own_ref, ...), custom_call_target="tpu_custom_call" | custom-call | tf_op jit(solution)/shard_map/warp/pallas_call | solution.py:303
  19.2 3.1 %collective-permute-start.10 = (f32[264,128]{1,0:T(8,128)}, f32[264,128]{1,0:T(8,128)S(1)}, u32[]{:S(2)}, u32[]{:S(2)}) collective-permute-start(f32[264,128]{1,0:T(8,128)} %get-tuple-element.40.refs_3_), channel_id=1, source_target_pairs={{0,3},{1,2},{2,1},{3,0},{4,7},{5,6},{6,5},{7,4},{8,11},{9,10},{10,... | collective-permute-start | bytes 405512 | tf_op jit(solution)/shard_map/ppermute | solution.py:476
  22.2 1.3 %collective-permute-start.11 = (f32[264,128]{1,0:T(8,128)}, f32[264,128]{1,0:T(8,128)S(1)}, u32[]{:S(2)}, u32[]{:S(2)}) collective-permute-start(f32[264,128]{1,0:T(8,128)} %get-tuple-element.41.refs_4_), channel_id=1, source_target_pairs={{0,4},{1,5},{2,6},{3,7},{4,0},{5,1},{6,2},{7,3},{8,12},{9,13},{10,... | collective-permute-start | bytes 405512 | tf_op jit(solution)/shard_map/ppermute | solution.py:476
  23.5 0.5 collective-permute-start.2
  24.5 0.7 collective-permute-done.1.refs_1_
  25.1 1.8 %collective-permute-start.13 = (f32[264,128]{1,0:T(8,128)}, f32[264,128]{1,0:T(8,128)S(1)}, u32[]{:S(2)}, u32[]{:S(2)}) collective-permute-start(f32[264,128]{1,0:T(8,128)} %get-tuple-element.43.refs_0_), channel_id=1, source_target_pairs={{0,6},{1,7},{2,4},{3,5},{4,2},{5,3},{6,0},{7,1},{8,14},{9,15},{10,... | collective-permute-start | bytes 405512 | tf_op jit(solution)/shard_map/ppermute | solution.py:476
  26.9 1.5 %collective-permute-done.2.refs_2_ = f32[256,128]{1,0:T(8,128)S(1)} collective-permute-done((f32[256,128]{1,0:T(8,128)}, f32[256,128]{1,0:T(8,128)S(1)}, u32[]{:S(2)}, u32[]{:S(2)}) %collective-permute-start.2) | collective-permute-done | bytes 131104 | tf_op jit(solution)/shard_map/ppermute | solution.py:476
  28.4 2.1 %collective-permute-start.14 = (f32[264,128]{1,0:T(8,128)}, f32[264,128]{1,0:T(8,128)S(1)}, u32[]{:S(2)}, u32[]{:S(2)}) collective-permute-start(f32[264,128]{1,0:T(8,128)} %get-tuple-element.44.refs_1_), channel_id=1, source_target_pairs={{0,7},{1,6},{2,5},{3,4},{4,3},{5,2},{6,1},{7,0},{8,15},{9,14},{10,... | collective-permute-start | bytes 405512 | tf_op jit(solution)/shard_map/ppermute | solution.py:476
  30.5 0.9 collective-permute-start.8
  31.4 1.1 %collective-permute-start.9 = (f32[264,128]{1,0:T(8,128)}, f32[264,128]{1,0:T(8,128)S(1)}, u32[]{:S(2)}, u32[]{:S(2)}) collective-permute-start(f32[264,128]{1,0:T(8,128)} %get-tuple-element.39.refs_2_), channel_id=1, source_target_pairs={{0,2},{1,3},{2,0},{3,1},{4,6},{5,7},{6,4},{7,5},{8,10},{9,11},{10,... | collective-permute-start | bytes 405512 | tf_op jit(solution)/shard_map/ppermute | solution.py:476
  32.5 0.6 collective-permute-start.3
  33.1 0.8 collective-permute-done.13.refs_6_
  33.9 0.8 collective-permute-start.4
  34.7 2.2 %collective-permute-done.14.refs_7_ = f32[264,128]{1,0:T(8,128)S(1)} collective-permute-done((f32[264,128]{1,0:T(8,128)}, f32[264,128]{1,0:T(8,128)S(1)}, u32[]{:S(2)}, u32[]{:S(2)}) %collective-permute-start.14) | collective-permute-done | bytes 135200 | tf_op jit(solution)/shard_map/ppermute | solution.py:476
  36.9 1.4 %collective-permute-start.5 = (f32[256,128]{1,0:T(8,128)}, f32[256,128]{1,0:T(8,128)S(1)}, u32[]{:S(2)}, u32[]{:S(2)}) collective-permute-start(f32[256,128]{1,0:T(8,128)} %get-tuple-element.34.refs_11_), channel_id=1, source_target_pairs={{0,5},{1,4},{2,7},{3,6},{4,1},{5,0},{6,3},{7,2},{8,13},{9,12},{10,... | collective-permute-start | bytes 393224 | tf_op jit(solution)/shard_map/ppermute | solution.py:476
  38.2 0.4 collective-permute-start.6
  38.7 1.1 %collective-permute-done.9.refs_2_ = f32[264,128]{1,0:T(8,128)S(1)} collective-permute-done((f32[264,128]{1,0:T(8,128)}, f32[264,128]{1,0:T(8,128)S(1)}, u32[]{:S(2)}, u32[]{:S(2)}) %collective-permute-start.9) | collective-permute-done | bytes 135200 | tf_op jit(solution)/shard_map/ppermute | solution.py:476
  39.8 1.9 %collective-permute-start.7 = (f32[256,128]{1,0:T(8,128)}, f32[256,128]{1,0:T(8,128)S(1)}, u32[]{:S(2)}, u32[]{:S(2)}) collective-permute-start(f32[256,128]{1,0:T(8,128)} %get-tuple-element.36.refs_3_), channel_id=1, source_target_pairs={{0,7},{1,6},{2,5},{3,4},{4,3},{5,2},{6,1},{7,0},{8,15},{9,14},{10,... | collective-permute-start | bytes 393224 | tf_op jit(solution)/shard_map/ppermute | solution.py:476
  41.7 2.8 %reduce_blocks.2 = (f32[512,128]{1,0:T(8,128)}, f32[8,128]{1,0:T(8,128)}) custom-call(s32[1]{0:T(128)} %bitcast.own_ref, s32[16,32]{1,0:T(8,128)} %dest_ref.7, s32[16,32]{1,0:T(8,128)} %dest_ref.7, f32[264,128]{1,0:T(8,128)} %get-tuple-element.37.refs_0_, f32[264,128]{1,0:T(8,128)} %copy-done.18, f32[264,128]{1,0:T(8,128)} %copy-done.19, ...), custom_call_target="tpu_custom_call" | custom-call | tf_op jit(solution)/shard_map/reduce_blocks/pallas_call | solution.py:391
  44.5 0.8 collective-permute-done.6.refs_6_
  45.3 2.9 %collective-permute-done.7.refs_7_ = f32[256,128]{1,0:T(8,128)S(1)} collective-permute-done((f32[256,128]{1,0:T(8,128)}, f32[256,128]{1,0:T(8,128)S(1)}, u32[]{:S(2)}, u32[]{:S(2)}) %collective-permute-start.7) | collective-permute-done | bytes 131104 | tf_op jit(solution)/shard_map/ppermute | solution.py:476
  48.3 0.6 copy-done.26
  48.9 2.8 %reduce_blocks.3 = (f32[512,128]{1,0:T(8,128)}, f32[8,128]{1,0:T(8,128)}) custom-call(s32[1]{0:T(128)} %bitcast.own_ref, s32[16,32]{1,0:T(8,128)} %dest_ref.7, s32[16,32]{1,0:T(8,128)} %dest_ref.7, f32[256,128]{1,0:T(8,128)} %get-tuple-element.29.refs_0_.refs_6_, f32[256,128]{1,0:T(8,128)} %copy-done.20, f32[256,128]{1,0:T(8,128)} %copy-done.21, ...), custom_call_target="tpu_custom_call" | custom-call | tf_op jit(solution)/shard_map/reduce_blocks/pallas_call | solution.py:391
  51.7 2.6 %collective-permute-start.19 = (f32[512,128]{1,0:T(8,128)}, f32[512,128]{1,0:T(8,128)S(1)}, u32[]{:S(2)}, u32[]{:S(2)}) collective-permute-start(f32[512,128]{1,0:T(8,128)} %get-tuple-element.48), channel_id=1, source_target_pairs={{0,8},{1,9},{2,10},{3,11},{4,12},{5,13},{6,14},{7,15},{8,0},{9,1},... | collective-permute-start | bytes 786440 | tf_op jit(solution)/shard_map/ppermute | solution.py:476
  54.3 17.7 %collective-permute-done.19 = f32[512,128]{1,0:T(8,128)S(1)} collective-permute-done((f32[512,128]{1,0:T(8,128)}, f32[512,128]{1,0:T(8,128)S(1)}, u32[]{:S(2)}, u32[]{:S(2)}) %collective-permute-start.19) | collective-permute-done | bytes 262176 | tf_op jit(solution)/shard_map/ppermute | solution.py:476
  72.0 1.0 add.14.refs_18_
  73.0 1.2 %collective-permute-start.28 = (f32[512,128]{1,0:T(8,128)S(1)}, f32[512,128]{1,0:T(8,128)S(1)}, u32[]{:S(2)}, u32[]{:S(2)}) collective-permute-start(f32[512,128]{1,0:T(8,128)S(1)} %add.14.refs_18_), channel_id=1, source_target_pairs={{0,2},{1,3},{2,0},{3,1},{4,6},{5,7},{6,4},{7,5},{8,10},{9,11},{10,... | collective-permute-start | bytes 786440 | tf_op jit(solution)/shard_map/ppermute | solution.py:476
  74.5 1.9 %collective-permute-start.27 = (f32[512,128]{1,0:T(8,128)S(1)}, f32[512,128]{1,0:T(8,128)S(1)}, u32[]{:S(2)}, u32[]{:S(2)}) collective-permute-start(f32[512,128]{1,0:T(8,128)S(1)} %add.14.refs_18_), channel_id=1, source_target_pairs={{0,1},{1,0},{2,3},{3,2},{4,5},{5,4},{6,7},{7,6},{8,9},{9,8},{10,11... | collective-permute-start | bytes 786440 | tf_op jit(solution)/shard_map/ppermute | solution.py:476
  76.4 1.2 %collective-permute-done.15 = f32[512,128]{1,0:T(8,128)S(1)} collective-permute-done((f32[512,128]{1,0:T(8,128)}, f32[512,128]{1,0:T(8,128)S(1)}, u32[]{:S(2)}, u32[]{:S(2)}) %collective-permute-start.15) | collective-permute-done | bytes 262176 | tf_op jit(solution)/shard_map/ppermute | solution.py:476
  77.6 1.0 add.13.refs_12_
  78.6 1.2 %collective-permute-start.16 = (f32[512,128]{1,0:T(8,128)S(1)}, f32[512,128]{1,0:T(8,128)S(1)}, u32[]{:S(2)}, u32[]{:S(2)}) collective-permute-start(f32[512,128]{1,0:T(8,128)S(1)} %add.13.refs_12_), channel_id=1, source_target_pairs={{0,2},{1,3},{2,0},{3,1},{4,6},{5,7},{6,4},{7,5},{8,10},{9,11},{10,... | collective-permute-start | bytes 786440 | tf_op jit(solution)/shard_map/ppermute | solution.py:476
  80.1 1.6 %collective-permute-start.23 = (f32[512,128]{1,0:T(8,128)S(1)}, f32[512,128]{1,0:T(8,128)S(1)}, u32[]{:S(2)}, u32[]{:S(2)}) collective-permute-start(f32[512,128]{1,0:T(8,128)S(1)} %add.13.refs_12_), channel_id=1, source_target_pairs={{0,1},{1,0},{2,3},{3,2},{4,5},{5,4},{6,7},{7,6},{8,9},{9,8},{10,11... | collective-permute-start | bytes 786440 | tf_op jit(solution)/shard_map/ppermute | solution.py:476
  81.8 0.9 collective-permute-done.20.refs_22_
  82.7 2.7 %collective-permute-start.29 = (f32[512,128]{1,0:T(8,128)S(1)}, f32[512,128]{1,0:T(8,128)S(1)}, u32[]{:S(2)}, u32[]{:S(2)}) collective-permute-start(f32[512,128]{1,0:T(8,128)S(1)} %collective-permute-done.28.refs_20_), channel_id=1, source_target_pairs={{0,1},{1,0},{2,3},{3,2},{4,5},{5,4},{6,7},{7,6},{8,9},{9,8},{10,11... | collective-permute-start | bytes 786440 | tf_op jit(solution)/shard_map/ppermute | solution.py:476
  85.5 1.6 %collective-permute-start.17 = (f32[512,128]{1,0:T(8,128)S(1)}, f32[512,128]{1,0:T(8,128)}, u32[]{:S(2)}, u32[]{:S(2)}) collective-permute-start(f32[512,128]{1,0:T(8,128)S(1)} %collective-permute-done.16.refs_14_), channel_id=1, source_target_pairs={{0,4},{1,5},{2,6},{3,7},{4,0},{5,1},{6,2},{7,3},{8,12},{9,13},{10,... | collective-permute-start | bytes 786440 | tf_op jit(solution)/shard_map/ppermute | solution.py:476
  87.1 1.2 %collective-permute-done.25.refs_16_ = f32[512,128]{1,0:T(8,128)S(1)} collective-permute-done((f32[512,128]{1,0:T(8,128)S(1)}, f32[512,128]{1,0:T(8,128)S(1)}, u32[]{:S(2)}, u32[]{:S(2)}) %collective-permute-start.25) | collective-permute-done | bytes 262176 | tf_op jit(solution)/shard_map/ppermute | solution.py:476
  88.3 2.6 %collective-permute-start.30 = (f32[512,128]{1,0:T(8,128)S(1)}, f32[512,128]{1,0:T(8,128)S(1)}, u32[]{:S(2)}, u32[]{:S(2)}) collective-permute-start(f32[512,128]{1,0:T(8,128)S(1)} %collective-permute-done.20.refs_22_), channel_id=1, source_target_pairs={{0,1},{1,0},{2,3},{3,2},{4,5},{5,4},{6,7},{7,6},{8,9},{9,8},{10,11... | collective-permute-start | bytes 786440 | tf_op jit(solution)/shard_map/ppermute | solution.py:476
  91.0 0.4 collective-permute-start.26
  91.4 1.8 %collective-permute-done.21.refs_6_ = f32[512,128]{1,0:T(8,128)S(1)} collective-permute-done((f32[512,128]{1,0:T(8,128)S(1)}, f32[512,128]{1,0:T(8,128)S(1)}, u32[]{:S(2)}, u32[]{:S(2)}) %collective-permute-start.21) | collective-permute-done | bytes 262176 | tf_op jit(solution)/shard_map/ppermute | solution.py:476
  93.2 0.8 collective-permute-start.22
  94.1 1.5 %collective-permute-start.18 = (f32[512,128]{1,0:T(8,128)}, f32[512,128]{1,0:T(8,128)}, u32[]{:S(2)}, u32[]{:S(2)}) collective-permute-start(f32[512,128]{1,0:T(8,128)} %collective-permute-done.17.refs_4_), channel_id=1, source_target_pairs={{0,1},{1,0},{2,3},{3,2},{4,5},{5,4},{6,7},{7,6},{8,9},{9,8},{10,11... | collective-permute-start | bytes 786440 | tf_op jit(solution)/shard_map/ppermute | solution.py:476
  95.7 0.6 copy-done.9
  96.4 3.9 %finish.2.refs_8_ = f32[8,4,128,128]{3,2,1,0:T(8,128)} custom-call(s32[1]{0:T(128)} %bitcast.own_ref, s32[16,32]{1,0:T(8,128)} %dest_ref.7, f32[8,128]{1,0:T(8,128)} %get-tuple-element.46.var_ref, f32[264,128]{1,0:T(8,128)} %get-tuple-element.37.refs_0_, f32[264,128]{1,0:T(8,128)} %get-tuple-element.38.refs_1_, f32[264,128]{1,0:T(8,128)} %get-tuple-element.39.refs_2_, ...), custom_call_target="tpu_custom_call" | custom-call | tf_op jit(solution)/shard_map/finish/pallas_call | solution.py:447
  100.3 2.3 %finish.3 = f32[8,4,128,128]{3,2,1,0:T(8,128)} custom-call(s32[1]{0:T(128)} %bitcast.own_ref, s32[16,32]{1,0:T(8,128)} %dest_ref.7, f32[8,128]{1,0:T(8,128)} %get-tuple-element.46.var_ref, f32[264,128]{1,0:T(8,128)} %get-tuple-element.43.refs_0_, f32[264,128]{1,0:T(8,128)} %get-tuple-element.44.refs_1_, ...), custom_call_target="tpu_custom_call", output_to_operand_aliasing={{}: (11, {})} | custom-call | tf_op jit(solution)/shard_map/finish/pallas_call | solution.py:447
  (78 shorter events, 1.7 us)
Async XLA Ops:
  7.8 4.3 %collective-permute-start = (f32[8,128]{1,0:T(8,128)}, f32[8,128]{1,0:T(8,128)S(1)}, u32[]{:S(2)}, u32[]{:S(2)}) collective-permute-start(f32[8,128]{1,0:T(8,128)} %get-tuple-element.28.refs_0_), channel_id=1, source_target_pairs={{0,8},{1,9},{2,10},{3,11},{4,12},{5,13},{6,14},{7,15},{8,0},{9,1},... | collective-permute-start | bytes 12296 | tf_op jit(solution)/shard_map/ppermute | solution.py:476
  19.2 11.3 %collective-permute-start.10 = (f32[264,128]{1,0:T(8,128)}, f32[264,128]{1,0:T(8,128)S(1)}, u32[]{:S(2)}, u32[]{:S(2)}) collective-permute-start(f32[264,128]{1,0:T(8,128)} %get-tuple-element.40.refs_3_), channel_id=1, source_target_pairs={{0,3},{1,2},{2,1},{3,0},{4,7},{5,6},{6,5},{7,4},{8,11},{9,10},{10,... | collective-permute-start | bytes 405512 | tf_op jit(solution)/shard_map/ppermute | solution.py:476
  22.2 9.1 %collective-permute-start.11 = (f32[264,128]{1,0:T(8,128)}, f32[264,128]{1,0:T(8,128)S(1)}, u32[]{:S(2)}, u32[]{:S(2)}) collective-permute-start(f32[264,128]{1,0:T(8,128)} %get-tuple-element.41.refs_4_), channel_id=1, source_target_pairs={{0,4},{1,5},{2,6},{3,7},{4,0},{5,1},{6,2},{7,3},{8,12},{9,13},{10,... | collective-permute-start | bytes 405512 | tf_op jit(solution)/shard_map/ppermute | solution.py:476
  23.5 1.6 %collective-permute-start.1 = (f32[256,128]{1,0:T(8,128)}, f32[256,128]{1,0:T(8,128)S(1)}, u32[]{:S(2)}, u32[]{:S(2)}) collective-permute-start(f32[256,128]{1,0:T(8,128)} %get-tuple-element.30.refs_7_), channel_id=1, source_target_pairs={{0,1},{1,0},{2,3},{3,2},{4,5},{5,4},{6,7},{7,6},{8,9},{9,8},{10,11... | collective-permute-start | bytes 393224 | tf_op jit(solution)/shard_map/ppermute | solution.py:476
  23.5 4.8 %collective-permute-start.2 = (f32[256,128]{1,0:T(8,128)}, f32[256,128]{1,0:T(8,128)S(1)}, u32[]{:S(2)}, u32[]{:S(2)}) collective-permute-start(f32[256,128]{1,0:T(8,128)} %get-tuple-element.31.refs_8_), channel_id=1, source_target_pairs={{0,2},{1,3},{2,0},{3,1},{4,6},{5,7},{6,4},{7,5},{8,10},{9,11},{10,... | collective-permute-start | bytes 393224 | tf_op jit(solution)/shard_map/ppermute | solution.py:476
  24.0 8.5 %collective-permute-start.12 = (f32[264,128]{1,0:T(8,128)}, f32[264,128]{1,0:T(8,128)S(1)}, u32[]{:S(2)}, u32[]{:S(2)}) collective-permute-start(f32[264,128]{1,0:T(8,128)} %get-tuple-element.42.refs_5_), channel_id=1, source_target_pairs={{0,5},{1,4},{2,7},{3,6},{4,1},{5,0},{6,3},{7,2},{8,13},{9,12},{10,... | collective-permute-start | bytes 405512 | tf_op jit(solution)/shard_map/ppermute | solution.py:476
  25.1 23.1 %copy-start.20 = (f32[256,128]{1,0:T(8,128)}, f32[256,128]{1,0:T(8,128)S(1)}, u32[]{:S(2)}) copy-start(f32[256,128]{1,0:T(8,128)S(1)} %collective-permute-done.1.refs_1_) | copy-start | bytes 393220
  25.1 8.8 %collective-permute-start.13 = (f32[264,128]{1,0:T(8,128)}, f32[264,128]{1,0:T(8,128)S(1)}, u32[]{:S(2)}, u32[]{:S(2)}) collective-permute-start(f32[264,128]{1,0:T(8,128)} %get-tuple-element.43.refs_0_), channel_id=1, source_target_pairs={{0,6},{1,7},{2,4},{3,5},{4,2},{5,3},{6,0},{7,1},{8,14},{9,15},{10,... | collective-permute-start | bytes 405512 | tf_op jit(solution)/shard_map/ppermute | solution.py:476
  28.4 19.9 %copy-start.21 = (f32[256,128]{1,0:T(8,128)}, f32[256,128]{1,0:T(8,128)S(1)}, u32[]{:S(2)}) copy-start(f32[256,128]{1,0:T(8,128)S(1)} %collective-permute-done.2.refs_2_) | copy-start | bytes 393220
  28.4 8.5 %collective-permute-start.14 = (f32[264,128]{1,0:T(8,128)}, f32[264,128]{1,0:T(8,128)S(1)}, u32[]{:S(2)}, u32[]{:S(2)}) collective-permute-start(f32[264,128]{1,0:T(8,128)} %get-tuple-element.44.refs_1_), channel_id=1, source_target_pairs={{0,7},{1,6},{2,5},{3,4},{4,3},{5,2},{6,1},{7,0},{8,15},{9,14},{10,... | collective-permute-start | bytes 405512 | tf_op jit(solution)/shard_map/ppermute | solution.py:476
  30.5 11.2 %copy-start.13 = (f32[264,128]{1,0:T(8,128)}, f32[264,128]{1,0:T(8,128)S(1)}, u32[]{:S(2)}) copy-start(f32[264,128]{1,0:T(8,128)S(1)} %collective-permute-done.10.refs_3_) | copy-start | bytes 405508
  30.5 7.7 %collective-permute-start.8 = (f32[264,128]{1,0:T(8,128)}, f32[264,128]{1,0:T(8,128)S(1)}, u32[]{:S(2)}, u32[]{:S(2)}) collective-permute-start(f32[264,128]{1,0:T(8,128)} %get-tuple-element.38.refs_1_), channel_id=1, source_target_pairs={{0,1},{1,0},{2,3},{3,2},{4,5},{5,4},{6,7},{7,6},{8,9},{9,8},{10,11... | collective-permute-start | bytes 405512 | tf_op jit(solution)/shard_map/ppermute | solution.py:476
  31.4 10.3 %copy-start.14 = (f32[264,128]{1,0:T(8,128)}, f32[264,128]{1,0:T(8,128)S(1)}, u32[]{:S(2)}) copy-start(f32[264,128]{1,0:T(8,128)S(1)} %collective-permute-done.11.refs_4_) | copy-start | bytes 405508
  31.4 8.4 %collective-permute-start.9 = (f32[264,128]{1,0:T(8,128)}, f32[264,128]{1,0:T(8,128)S(1)}, u32[]{:S(2)}, u32[]{:S(2)}) collective-permute-start(f32[264,128]{1,0:T(8,128)} %get-tuple-element.39.refs_2_), channel_id=1, source_target_pairs={{0,2},{1,3},{2,0},{3,1},{4,6},{5,7},{6,4},{7,5},{8,10},{9,11},{10,... | collective-permute-start | bytes 405512 | tf_op jit(solution)/shard_map/ppermute | solution.py:476
  32.5 9.1 %copy-start.15 = (f32[264,128]{1,0:T(8,128)}, f32[264,128]{1,0:T(8,128)S(1)}, u32[]{:S(2)}) copy-start(f32[264,128]{1,0:T(8,128)S(1)} %collective-permute-done.12.refs_5_) | copy-start | bytes 405508
  32.5 12.0 %collective-permute-start.3 = (f32[256,128]{1,0:T(8,128)}, f32[256,128]{1,0:T(8,128)S(1)}, u32[]{:S(2)}, u32[]{:S(2)}) collective-permute-start(f32[256,128]{1,0:T(8,128)} %get-tuple-element.32.refs_9_), channel_id=1, source_target_pairs={{0,3},{1,2},{2,1},{3,0},{4,7},{5,6},{6,5},{7,4},{8,11},{9,10},{10,... | collective-permute-start | bytes 393224 | tf_op jit(solution)/shard_map/ppermute | solution.py:476
  33.9 7.7 %copy-start.16 = (f32[264,128]{1,0:T(8,128)}, f32[264,128]{1,0:T(8,128)S(1)}, u32[]{:S(2)}) copy-start(f32[264,128]{1,0:T(8,128)S(1)} %collective-permute-done.13.refs_6_) | copy-start | bytes 405508
  33.9 10.6 %collective-permute-start.4 = (f32[256,128]{1,0:T(8,128)}, f32[256,128]{1,0:T(8,128)S(1)}, u32[]{:S(2)}, u32[]{:S(2)}) collective-permute-start(f32[256,128]{1,0:T(8,128)} %get-tuple-element.33.refs_10_), channel_id=1, source_target_pairs={{0,4},{1,5},{2,6},{3,7},{4,0},{5,1},{6,2},{7,3},{8,12},{9,13},{10,... | collective-permute-start | bytes 393224 | tf_op jit(solution)/shard_map/ppermute | solution.py:476
  36.9 4.8 %copy-start.17 = (f32[264,128]{1,0:T(8,128)}, f32[264,128]{1,0:T(8,128)S(1)}, u32[]{:S(2)}) copy-start(f32[264,128]{1,0:T(8,128)S(1)} %collective-permute-done.14.refs_7_) | copy-start | bytes 405508
  36.9 7.6 %collective-permute-start.5 = (f32[256,128]{1,0:T(8,128)}, f32[256,128]{1,0:T(8,128)S(1)}, u32[]{:S(2)}, u32[]{:S(2)}) collective-permute-start(f32[256,128]{1,0:T(8,128)} %get-tuple-element.34.refs_11_), channel_id=1, source_target_pairs={{0,5},{1,4},{2,7},{3,6},{4,1},{5,0},{6,3},{7,2},{8,13},{9,12},{10,... | collective-permute-start | bytes 393224 | tf_op jit(solution)/shard_map/ppermute | solution.py:476
  38.2 7.1 %collective-permute-start.6 = (f32[256,128]{1,0:T(8,128)}, f32[256,128]{1,0:T(8,128)S(1)}, u32[]{:S(2)}, u32[]{:S(2)}) collective-permute-start(f32[256,128]{1,0:T(8,128)} %get-tuple-element.35.refs_2_), channel_id=1, source_target_pairs={{0,6},{1,7},{2,4},{3,5},{4,2},{5,3},{6,0},{7,1},{8,14},{9,15},{10,... | collective-permute-start | bytes 393224 | tf_op jit(solution)/shard_map/ppermute | solution.py:476
  39.8 8.5 %collective-permute-start.7 = (f32[256,128]{1,0:T(8,128)}, f32[256,128]{1,0:T(8,128)S(1)}, u32[]{:S(2)}, u32[]{:S(2)}) collective-permute-start(f32[256,128]{1,0:T(8,128)} %get-tuple-element.36.refs_3_), channel_id=1, source_target_pairs={{0,7},{1,6},{2,5},{3,4},{4,3},{5,2},{6,1},{7,0},{8,15},{9,14},{10,... | collective-permute-start | bytes 393224 | tf_op jit(solution)/shard_map/ppermute | solution.py:476
  51.7 20.3 %collective-permute-start.19 = (f32[512,128]{1,0:T(8,128)}, f32[512,128]{1,0:T(8,128)S(1)}, u32[]{:S(2)}, u32[]{:S(2)}) collective-permute-start(f32[512,128]{1,0:T(8,128)} %get-tuple-element.48), channel_id=1, source_target_pairs={{0,8},{1,9},{2,10},{3,11},{4,12},{5,13},{6,14},{7,15},{8,0},{9,1},... | collective-permute-start | bytes 786440 | tf_op jit(solution)/shard_map/ppermute | solution.py:476
  54.2 23.4 %collective-permute-start.15 = (f32[512,128]{1,0:T(8,128)}, f32[512,128]{1,0:T(8,128)S(1)}, u32[]{:S(2)}, u32[]{:S(2)}) collective-permute-start(f32[512,128]{1,0:T(8,128)} %get-tuple-element.47), channel_id=1, source_target_pairs={{0,8},{1,9},{2,10},{3,11},{4,12},{5,13},{6,14},{7,15},{8,0},{9,1},... | collective-permute-start | bytes 786440 | tf_op jit(solution)/shard_map/ppermute | solution.py:476
  73.0 22.6 %copy-start = (f32[512,128]{1,0:T(8,128)}, f32[512,128]{1,0:T(8,128)S(1)}, u32[]{:S(2)}) copy-start(f32[512,128]{1,0:T(8,128)S(1)} %add.14.refs_18_) | copy-start | bytes 786436
  73.0 7.2 %collective-permute-start.28 = (f32[512,128]{1,0:T(8,128)S(1)}, f32[512,128]{1,0:T(8,128)S(1)}, u32[]{:S(2)}, u32[]{:S(2)}) collective-permute-start(f32[512,128]{1,0:T(8,128)S(1)} %add.14.refs_18_), channel_id=1, source_target_pairs={{0,2},{1,3},{2,0},{3,1},{4,6},{5,7},{6,4},{7,5},{8,10},{9,11},{10,... | collective-permute-start | bytes 786440 | tf_op jit(solution)/shard_map/ppermute | solution.py:476
  74.2 8.5 %collective-permute-start.20 = (f32[512,128]{1,0:T(8,128)S(1)}, f32[512,128]{1,0:T(8,128)S(1)}, u32[]{:S(2)}, u32[]{:S(2)}) collective-permute-start(f32[512,128]{1,0:T(8,128)S(1)} %add.14.refs_18_), channel_id=1, source_target_pairs={{0,4},{1,5},{2,6},{3,7},{4,0},{5,1},{6,2},{7,3},{8,12},{9,13},{10,... | collective-permute-start | bytes 786440 | tf_op jit(solution)/shard_map/ppermute | solution.py:476
  74.5 10.8 %collective-permute-start.27 = (f32[512,128]{1,0:T(8,128)S(1)}, f32[512,128]{1,0:T(8,128)S(1)}, u32[]{:S(2)}, u32[]{:S(2)}) collective-permute-start(f32[512,128]{1,0:T(8,128)S(1)} %add.14.refs_18_), channel_id=1, source_target_pairs={{0,1},{1,0},{2,3},{3,2},{4,5},{5,4},{6,7},{7,6},{8,9},{9,8},{10,11... | collective-permute-start | bytes 786440 | tf_op jit(solution)/shard_map/ppermute | solution.py:476
  78.6 17.0 %copy-start.1 = (f32[512,128]{1,0:T(8,128)}, f32[512,128]{1,0:T(8,128)S(1)}, u32[]{:S(2)}) copy-start(f32[512,128]{1,0:T(8,128)S(1)} %add.13.refs_12_) | copy-start | bytes 786436
  78.6 6.9 %collective-permute-start.16 = (f32[512,128]{1,0:T(8,128)S(1)}, f32[512,128]{1,0:T(8,128)S(1)}, u32[]{:S(2)}, u32[]{:S(2)}) collective-permute-start(f32[512,128]{1,0:T(8,128)S(1)} %add.13.refs_12_), channel_id=1, source_target_pairs={{0,2},{1,3},{2,0},{3,1},{4,6},{5,7},{6,4},{7,5},{8,10},{9,11},{10,... | collective-permute-start | bytes 786440 | tf_op jit(solution)/shard_map/ppermute | solution.py:476
  79.8 8.5 %collective-permute-start.25 = (f32[512,128]{1,0:T(8,128)S(1)}, f32[512,128]{1,0:T(8,128)S(1)}, u32[]{:S(2)}, u32[]{:S(2)}) collective-permute-start(f32[512,128]{1,0:T(8,128)S(1)} %add.13.refs_12_), channel_id=1, source_target_pairs={{0,4},{1,5},{2,6},{3,7},{4,0},{5,1},{6,2},{7,3},{8,12},{9,13},{10,... | collective-permute-start | bytes 786440 | tf_op jit(solution)/shard_map/ppermute | solution.py:476
  80.1 15.5 %copy-start.2 = (f32[512,128]{1,0:T(8,128)}, f32[512,128]{1,0:T(8,128)S(1)}, u32[]{:S(2)}) copy-start(f32[512,128]{1,0:T(8,128)S(1)} %collective-permute-done.28.refs_20_) | copy-start | bytes 786436
  80.1 10.7 %collective-permute-start.23 = (f32[512,128]{1,0:T(8,128)S(1)}, f32[512,128]{1,0:T(8,128)S(1)}, u32[]{:S(2)}, u32[]{:S(2)}) collective-permute-start(f32[512,128]{1,0:T(8,128)S(1)} %add.13.refs_12_), channel_id=1, source_target_pairs={{0,1},{1,0},{2,3},{3,2},{4,5},{5,4},{6,7},{7,6},{8,9},{9,8},{10,11... | collective-permute-start | bytes 786440 | tf_op jit(solution)/shard_map/ppermute | solution.py:476
  82.7 13.0 %copy-start.3 = (f32[512,128]{1,0:T(8,128)}, f32[512,128]{1,0:T(8,128)S(1)}, u32[]{:S(2)}) copy-start(f32[512,128]{1,0:T(8,128)S(1)} %collective-permute-done.20.refs_22_) | copy-start | bytes 786436
  82.7 8.3 %collective-permute-start.29 = (f32[512,128]{1,0:T(8,128)S(1)}, f32[512,128]{1,0:T(8,128)S(1)}, u32[]{:S(2)}, u32[]{:S(2)}) collective-permute-start(f32[512,128]{1,0:T(8,128)S(1)} %collective-permute-done.28.refs_20_), channel_id=1, source_target_pairs={{0,1},{1,0},{2,3},{3,2},{4,5},{5,4},{6,7},{7,6},{8,9},{9,8},{10,11... | collective-permute-start | bytes 786440 | tf_op jit(solution)/shard_map/ppermute | solution.py:476
  85.3 10.3 %copy-start.4 = (f32[512,128]{1,0:T(8,128)}, f32[512,128]{1,0:T(8,128)S(1)}, u32[]{:S(2)}) copy-start(f32[512,128]{1,0:T(8,128)S(1)} %collective-permute-done.27.refs_19_) | copy-start | bytes 786436
  85.3 7.9 %collective-permute-start.21 = (f32[512,128]{1,0:T(8,128)S(1)}, f32[512,128]{1,0:T(8,128)S(1)}, u32[]{:S(2)}, u32[]{:S(2)}) collective-permute-start(f32[512,128]{1,0:T(8,128)S(1)} %collective-permute-done.20.refs_22_), channel_id=1, source_target_pairs={{0,2},{1,3},{2,0},{3,1},{4,6},{5,7},{6,4},{7,5},{8,10},{9,11},{10,... | collective-permute-start | bytes 786440 | tf_op jit(solution)/shard_map/ppermute | solution.py:476
  85.5 10.1 %copy-start.5 = (f32[512,128]{1,0:T(8,128)}, f32[512,128]{1,0:T(8,128)S(1)}, u32[]{:S(2)}) copy-start(f32[512,128]{1,0:T(8,128)S(1)} %collective-permute-done.16.refs_14_) | copy-start | bytes 786436
  85.5 8.5 %collective-permute-start.17 = (f32[512,128]{1,0:T(8,128)S(1)}, f32[512,128]{1,0:T(8,128)}, u32[]{:S(2)}, u32[]{:S(2)}) collective-permute-start(f32[512,128]{1,0:T(8,128)S(1)} %collective-permute-done.16.refs_14_), channel_id=1, source_target_pairs={{0,4},{1,5},{2,6},{3,7},{4,0},{5,1},{6,2},{7,3},{8,12},{9,13},{10,... | collective-permute-start | bytes 786440 | tf_op jit(solution)/shard_map/ppermute | solution.py:476
  88.3 7.4 %copy-start.6 = (f32[512,128]{1,0:T(8,128)}, f32[512,128]{1,0:T(8,128)S(1)}, u32[]{:S(2)}) copy-start(f32[512,128]{1,0:T(8,128)S(1)} %collective-permute-done.25.refs_16_) | copy-start | bytes 786436
  88.3 7.3 %collective-permute-start.30 = (f32[512,128]{1,0:T(8,128)S(1)}, f32[512,128]{1,0:T(8,128)S(1)}, u32[]{:S(2)}, u32[]{:S(2)}) collective-permute-start(f32[512,128]{1,0:T(8,128)S(1)} %collective-permute-done.20.refs_22_), channel_id=1, source_target_pairs={{0,1},{1,0},{2,3},{3,2},{4,5},{5,4},{6,7},{7,6},{8,9},{9,8},{10,11... | collective-permute-start | bytes 786440 | tf_op jit(solution)/shard_map/ppermute | solution.py:476
  90.9 4.8 %copy-start.7 = (f32[512,128]{1,0:T(8,128)}, f32[512,128]{1,0:T(8,128)S(1)}, u32[]{:S(2)}) copy-start(f32[512,128]{1,0:T(8,128)S(1)} %collective-permute-done.23.refs_13_) | copy-start | bytes 786436
  90.9 4.7 %collective-permute-start.24 = (f32[512,128]{1,0:T(8,128)S(1)}, f32[512,128]{1,0:T(8,128)S(1)}, u32[]{:S(2)}, u32[]{:S(2)}) collective-permute-start(f32[512,128]{1,0:T(8,128)S(1)} %collective-permute-done.16.refs_14_), channel_id=1, source_target_pairs={{0,1},{1,0},{2,3},{3,2},{4,5},{5,4},{6,7},{7,6},{8,9},{9,8},{10,11... | collective-permute-start | bytes 786440 | tf_op jit(solution)/shard_map/ppermute | solution.py:476
  91.0 4.7 %copy-start.8 = (f32[512,128]{1,0:T(8,128)}, f32[512,128]{1,0:T(8,128)S(1)}, u32[]{:S(2)}) copy-start(f32[512,128]{1,0:T(8,128)S(1)} %collective-permute-done.29.refs_21_) | copy-start | bytes 786436
  91.0 4.6 %collective-permute-start.26 = (f32[512,128]{1,0:T(8,128)S(1)}, f32[512,128]{1,0:T(8,128)S(1)}, u32[]{:S(2)}, u32[]{:S(2)}) collective-permute-start(f32[512,128]{1,0:T(8,128)S(1)} %collective-permute-done.25.refs_16_), channel_id=1, source_target_pairs={{0,1},{1,0},{2,3},{3,2},{4,5},{5,4},{6,7},{7,6},{8,9},{9,8},{10,11... | collective-permute-start | bytes 786440 | tf_op jit(solution)/shard_map/ppermute | solution.py:476
  93.2 7.1 %copy-start.12 = (f32[512,128]{1,0:T(8,128)}, f32[512,128]{1,0:T(8,128)S(1)}, u32[]{:S(2)}) copy-start(f32[512,128]{1,0:T(8,128)S(1)} %collective-permute-done.21.refs_6_) | copy-start | bytes 786436
  93.2 7.1 %collective-permute-start.22 = (f32[512,128]{1,0:T(8,128)S(1)}, f32[512,128]{1,0:T(8,128)}, u32[]{:S(2)}, u32[]{:S(2)}) collective-permute-start(f32[512,128]{1,0:T(8,128)S(1)} %collective-permute-done.21.refs_6_), channel_id=1, source_target_pairs={{0,1},{1,0},{2,3},{3,2},{4,5},{5,4},{6,7},{7,6},{8,9},{9,8},{10,11... | collective-permute-start | bytes 786440 | tf_op jit(solution)/shard_map/ppermute | solution.py:476
  94.1 6.3 %collective-permute-start.18 = (f32[512,128]{1,0:T(8,128)}, f32[512,128]{1,0:T(8,128)}, u32[]{:S(2)}, u32[]{:S(2)}) collective-permute-start(f32[512,128]{1,0:T(8,128)} %collective-permute-done.17.refs_4_), channel_id=1, source_target_pairs={{0,1},{1,0},{2,3},{3,2},{4,5},{5,4},{6,7},{7,6},{8,9},{9,8},{10,11... | collective-permute-start | bytes 786440 | tf_op jit(solution)/shard_map/ppermute | solution.py:476
  (11 other events, 23.2 us)
